TPU v7x, 32 devices: a whole 2x2x4 slice. The times are simulated.
32 devices in a mesh: head: 4 (over y, x), blk: 8 (over z, core).
Axes of the slice: x: 2, y: 2, z: 4, core: 2. Of those that a mesh axis runs over, the one named last changes fastest.
Arguments:
- tokens: bfloat16 [8, 6144, 512], P('blk', 'head'), may hold values from -6 to 6
- cotangent: bfloat16 [8, 6144, 512], P('blk', 'head'), may hold values from -6 to 6
- doc_lengths: int32 [49], replicated, may hold values from 1 to 62, 1536 in all
- norm_gain1: bfloat16 [512], P(('head', 'blk')), may hold values from 0.25 to 1.75
- w_qkv: bfloat16 [512, 1536], P('head', 'blk'), may hold values from -0.25 to 0.25
- w_out: bfloat16 [512, 512], P('head', 'blk'), may hold values from -0.75 to 0.75
- b_out: bfloat16 [512], P(('head', 'blk')), may hold values from -3 to 3
- norm_gain2: bfloat16 [512], P(('head', 'blk')), may hold values from 0.25 to 1.75
- w_in: bfloat16 [512, 2048], P('head', 'blk'), may hold values from -0.25 to 0.25
- b_in: bfloat16 [2048], P(('head', 'blk')), may hold values from -3 to 3
- w_down: bfloat16 [2048, 512], P('head', 'blk'), may hold values from -0.125 to 0.125
- b_down: bfloat16 [512], P(('head', 'blk')), may hold values from -3 to 3
- w_sort: bfloat16 [512, 64], P('head', 'blk'), may hold values from -6 to 6
Outputs:
- output: bfloat16 [8, 6144, 512], P('blk', 'head')
- input_grad: float32 [8, 6144, 512], P('blk', 'head')
- grad_norm_gain1: float32 [512], P(('head', 'blk'))
- grad_w_qkv: float32 [512, 1536], P('head', 'blk')
- grad_w_out: float32 [512, 512], P('head', 'blk')
- grad_b_out: float32 [512], P(('head', 'blk'))
- grad_norm_gain2: float32 [512], P(('head', 'blk'))
- grad_w_in: float32 [512, 2048], P('head', 'blk')
- grad_b_in: float32 [2048], P(('head', 'blk'))
- grad_w_down: float32 [2048, 512], P('head', 'blk')
- grad_b_down: float32 [512], P(('head', 'blk'))
- grad_w_sort: float32 [512, 64], P('head', 'blk')
Inputs may be any that keep to these rules, and one draw needn't show every extreme that they name: `doc_lengths`: document lengths in blocks of 32 tokens; they sum to 1536 and the longest has exactly 62 blocks.
All inputs are finite; a program needn't handle non-finite values.
Results may differ from a plain program's by a relative error of at most 0.02.
The roundings to bfloat16 on the way count: a program that leaves them out, or rounds other values in their place, can miss the bound.
Values may be sent and summed in bfloat16 or wider, within the bound.
No kernel may reach another device: no remote copies, remote signals or barrier semaphores. Data moves between devices by JAX's collectives and lax.ppermute only.
A program may use at most 192 MiB of HBM per device.

v0:
```python
import jax
import jax.numpy as jnp
from jax import lax
from jax.sharding import PartitionSpec as P

D = 512
HEADS = 8
HEAD_DIM = 64
BLOCK = 32
SINK_ITERS = 8
DOC_MOST = 62


PRECISE = lax.Precision.HIGHEST
EPSILON = 1e-05
NEGATIVE = -1e30


def shifted_2(value, axis, steps):
    count = lax.axis_size(axis)
    leading, last = (max(0, -steps), min(count, count - steps))
    return lax.ppermute(value, axis, [(source, source + steps) for source in range(leading, last)])


def layer_norm(values, gain):
    centre = values - jnp.mean(values, axis=-1, keepdims=True)
    spread = jnp.mean(centre * centre, axis=-1, keepdims=True)
    return centre * lax.rsqrt(spread + EPSILON) * gain


def gelu_tanh(values):
    return jax.nn.gelu(values, approximate=True)


def masked_logsum(values, permitted_blocks, axis):
    alive = jnp.any(permitted_blocks, axis=axis, keepdims=True)
    highest = jnp.max(jnp.where(permitted_blocks, values, NEGATIVE), axis=axis, keepdims=True)
    highest = jnp.where(alive, highest, 0.0)
    shifted = jnp.exp(jnp.where(permitted_blocks, values, highest) - highest)
    total = jnp.sum(jnp.where(permitted_blocks, shifted, 0.0), axis=axis, keepdims=True)
    return jnp.where(alive, highest + jnp.log(jnp.where(alive, total, 1.0)), 0.0)


def balanced_transport_plan(block_logits, permitted_blocks):
    values = jnp.where(permitted_blocks, block_logits, 0.0)
    for repeat in range(SINK_ITERS):
        values = jnp.where(
            permitted_blocks, values - masked_logsum(values, permitted_blocks, 2), 0.0
        )
        values = jnp.where(
            permitted_blocks, values - masked_logsum(values, permitted_blocks, 1), 0.0
        )
    return jnp.where(permitted_blocks, jnp.exp(values), 0.0)


def block_documents(first, number, doc_lengths, total):
    position = first + jnp.arange(number, dtype=jnp.int32)
    doc_ends = jnp.cumsum(doc_lengths, dtype=jnp.int32)
    ended = jnp.sum(
        (doc_ends[None, :] <= position[:, None]).astype(jnp.int32), axis=1, dtype=jnp.int32
    )
    inside = (position >= 0) & (position < total)
    return jnp.where(inside, ended, -1)


def sort_allowed(doc_ids):
    number = doc_ids.shape[0]
    later = jnp.arange(number)[:, None] > jnp.arange(number)[None, :]
    return (doc_ids[:, None] == doc_ids[None, :]) & (doc_ids[:, None] >= 0) & later


def lattice(vector):
    return vector.reshape(1, 1, -1)


def per_device(
    tokens,
    cotangent,
    doc_lengths,
    norm_gain1,
    w_qkv,
    w_out,
    b_out,
    norm_gain2,
    w_in,
    b_in,
    w_down,
    b_down,
    w_sort,
):
    head_count = lax.axis_size("head")
    cycle_count = lax.axis_size("blk")
    local_heads = HEADS // head_count
    attend_range = DOC_MOST - 1
    scale = HEAD_DIM ** (-0.5)
    first_pass = (
        lax.all_gather(w_qkv, "blk", axis=1, tiled=True),
        lax.all_gather(w_out, "blk", axis=1, tiled=True),
        lax.all_gather(w_in, "blk", axis=1, tiled=True),
        lax.all_gather(w_down, "blk", axis=1, tiled=True),
        lax.all_gather(w_sort, "blk", axis=1, tiled=True),
        lax.all_gather(lattice(norm_gain1), "blk", axis=1, tiled=True),
        lax.all_gather(lattice(b_out), "blk", axis=1, tiled=True),
        lax.all_gather(lattice(norm_gain2), "blk", axis=1, tiled=True),
        lax.all_gather(lattice(b_in), "blk", axis=1, tiled=True),
        lax.all_gather(lattice(b_down), "blk", axis=1, tiled=True),
    )
    second_pass = (
        lax.all_gather(first_pass[0], "head", axis=0, tiled=True),
        lax.all_gather(first_pass[1], "head", axis=0, tiled=True),
        lax.all_gather(first_pass[2], "head", axis=0, tiled=True),
        lax.all_gather(first_pass[3], "head", axis=0, tiled=True),
        lax.all_gather(first_pass[5], "head", axis=0, tiled=True),
        lax.all_gather(first_pass[6], "head", axis=0, tiled=True),
        lax.all_gather(first_pass[7], "head", axis=0, tiled=True),
        lax.all_gather(first_pass[8], "head", axis=0, tiled=True),
        lax.all_gather(first_pass[9], "head", axis=0, tiled=True),
    )
    weight_qkv = second_pass[0]
    weight_out = second_pass[1]
    weight_in = second_pass[2]
    weight_down = second_pass[3]
    gain_one = second_pass[4].reshape(-1).astype(jnp.float32)
    bias_out = second_pass[5].reshape(-1).astype(jnp.float32)
    gain_two = second_pass[6].reshape(-1).astype(jnp.float32)
    bias_in = second_pass[7].reshape(-1).astype(jnp.float32)
    bias_down = second_pass[8].reshape(-1).astype(jnp.float32)
    sort_weight = first_pass[4].astype(jnp.float32).reshape(local_heads, HEAD_DIM, HEAD_DIM)
    resid = tokens[0].astype(jnp.float32)
    tok_rows = resid.shape[0]
    normed_f, norm_one_back = jax.vjp(layer_norm, resid, gain_one)
    normed = normed_f.astype(jnp.bfloat16)
    qkv = jnp.dot(normed, weight_qkv, preferred_element_type=jnp.float32).astype(jnp.bfloat16)
    regrouped = lax.all_to_all(
        qkv.reshape(tok_rows, HEADS, 3 * HEAD_DIM), "head", split_axis=1, concat_axis=0, tiled=True
    )
    span_rows = regrouped.shape[0]
    document_span_blocks = span_rows // BLOCK
    blocks = regrouped.reshape(document_span_blocks, BLOCK, local_heads, 3 * HEAD_DIM)
    query = blocks[..., :HEAD_DIM]
    key_local = blocks[..., HEAD_DIM : 2 * HEAD_DIM]
    value_local = blocks[..., 2 * HEAD_DIM :]
    keyval = blocks[..., HEAD_DIM:]
    means = jnp.concatenate(
        [
            jnp.mean(query.astype(jnp.float32), axis=1),
            jnp.mean(key_local.astype(jnp.float32), axis=1),
        ],
        axis=-1,
    )
    earlier_means = shifted_2(means[document_span_blocks - attend_range :], "blk", 1)
    beside_all = jnp.concatenate([earlier_means, means], axis=0)
    earlier = shifted_2(keyval[document_span_blocks - attend_range :], "blk", 1)
    context = jnp.concatenate([earlier, keyval], axis=0)
    doc_ids = block_documents(
        lax.axis_index("blk") * document_span_blocks - attend_range,
        document_span_blocks + attend_range,
        doc_lengths,
        document_span_blocks * cycle_count,
    )
    permitted_blocks = sort_allowed(doc_ids)

    def sort_step(outer, weight):
        block_logits = jnp.einsum(
            "nhi,hij,mhj->hnm",
            outer[..., :HEAD_DIM],
            weight,
            outer[..., HEAD_DIM:],
            precision=PRECISE,
        )
        permutation_every_head = balanced_transport_plan(block_logits, permitted_blocks[None])
        return permutation_every_head[
            :,
            attend_range : attend_range + document_span_blocks,
            : attend_range + document_span_blocks,
        ]

    block_permutation, sort_back = jax.vjp(sort_step, beside_all, sort_weight)
    sorting_low = block_permutation.astype(jnp.bfloat16)
    sorted_kv = jnp.einsum(
        "hnm,mbhe->nbhe", sorting_low, context, preferred_element_type=jnp.float32
    ).astype(jnp.bfloat16)
    key_sorted = sorted_kv[..., :HEAD_DIM]
    value_sorted = sorted_kv[..., HEAD_DIM:]
    live_rows = jnp.any(
        permitted_blocks[
            attend_range : attend_range + document_span_blocks,
            : attend_range + document_span_blocks,
        ],
        axis=1,
    )
    causal = jnp.arange(BLOCK)[:, None] >= jnp.arange(BLOCK)[None, :]
    local_scores = (
        jnp.einsum("nbhd,nchd->nhbc", query, key_local, preferred_element_type=jnp.float32) * scale
    )
    sorted_scores = (
        jnp.einsum("nbhd,nchd->nhbc", query, key_sorted, preferred_element_type=jnp.float32) * scale
    )
    scores = jnp.concatenate(
        [
            jnp.where(causal, local_scores, NEGATIVE),
            jnp.where(live_rows[:, None, None, None], sorted_scores, NEGATIVE),
        ],
        axis=-1,
    )
    highest = jnp.max(scores, axis=-1, keepdims=True)
    log_total = highest + jnp.log(jnp.sum(jnp.exp(scores - highest), axis=-1, keepdims=True))
    weights = jnp.exp(scores - log_total)
    weights_low = weights.astype(jnp.bfloat16)
    mixed = jnp.einsum(
        "nhbc,nche->nbhe", weights_low[..., :BLOCK], value_local, preferred_element_type=jnp.float32
    )
    mixed = mixed + jnp.einsum(
        "nhbc,nche->nbhe",
        weights_low[..., BLOCK:],
        value_sorted,
        preferred_element_type=jnp.float32,
    )
    returned = lax.all_to_all(
        mixed.astype(jnp.bfloat16).reshape(span_rows, local_heads, HEAD_DIM),
        "head",
        split_axis=0,
        concat_axis=1,
        tiled=True,
    )
    attended = returned.reshape(tok_rows, D)
    middle = resid + jnp.dot(attended, weight_out, preferred_element_type=jnp.float32) + bias_out
    normed_two_f, norm_two_back = jax.vjp(layer_norm, middle, gain_two)
    normed_two = normed_two_f.astype(jnp.bfloat16)
    pre = jnp.dot(normed_two, weight_in, preferred_element_type=jnp.float32) + bias_in
    act_out, act_back = jax.vjp(gelu_tanh, pre)
    hidden = act_out.astype(jnp.bfloat16)
    output = middle + jnp.dot(hidden, weight_down, preferred_element_type=jnp.float32) + bias_down
    upstream = cotangent[0]
    upstream_f = upstream.astype(jnp.float32)
    grad_down = jnp.einsum("tf,td->fd", hidden, upstream, preferred_element_type=jnp.float32)
    grad_bias_down = jnp.sum(upstream_f, axis=0)
    grad_hidden = jnp.einsum("td,fd->tf", upstream, weight_down, preferred_element_type=jnp.float32)
    grad_pre = act_back(grad_hidden)[0].astype(jnp.bfloat16)
    grad_in = jnp.einsum("td,tf->df", normed_two, grad_pre, preferred_element_type=jnp.float32)
    grad_bias_in = jnp.sum(grad_pre.astype(jnp.float32), axis=0)
    grad_normed_two = jnp.einsum(
        "tf,df->td", grad_pre, weight_in, preferred_element_type=jnp.float32
    )
    grad_middle_norm, grad_gain_two = norm_two_back(grad_normed_two)
    grad_middle = upstream_f + grad_middle_norm
    grad_branch = grad_middle.astype(jnp.bfloat16)
    grad_out = jnp.einsum("td,te->de", attended, grad_branch, preferred_element_type=jnp.float32)
    grad_bias_out = jnp.sum(grad_branch.astype(jnp.float32), axis=0)
    grad_attended = jnp.einsum(
        "te,de->td", grad_branch, weight_out, preferred_element_type=jnp.float32
    ).astype(jnp.bfloat16)
    grad_mixed = lax.all_to_all(
        grad_attended.reshape(tok_rows, HEADS, HEAD_DIM),
        "head",
        split_axis=1,
        concat_axis=0,
        tiled=True,
    )
    grad_mixed = grad_mixed.reshape(document_span_blocks, BLOCK, local_heads, HEAD_DIM)
    grad_w_local = jnp.einsum(
        "nbhe,nche->nhbc", grad_mixed, value_local, preferred_element_type=jnp.float32
    )
    grad_w_sorted = jnp.einsum(
        "nbhe,nche->nhbc", grad_mixed, value_sorted, preferred_element_type=jnp.float32
    )
    grad_weights = jnp.concatenate([grad_w_local, grad_w_sorted], axis=-1)
    grad_scores = weights * (grad_weights - jnp.sum(weights * grad_weights, axis=-1, keepdims=True))
    grad_scores = grad_scores.astype(jnp.bfloat16)
    grad_s_local = grad_scores[..., :BLOCK]
    grad_s_sorted = grad_scores[..., BLOCK:]
    grad_query = jnp.einsum(
        "nhbc,nchd->nbhd", grad_s_local, key_local, preferred_element_type=jnp.float32
    )
    grad_query = (
        grad_query
        + jnp.einsum(
            "nhbc,nchd->nbhd", grad_s_sorted, key_sorted, preferred_element_type=jnp.float32
        )
    ) * scale
    grad_key_local = (
        jnp.einsum("nhbc,nbhd->nchd", grad_s_local, query, preferred_element_type=jnp.float32)
        * scale
    )
    grad_value_local = jnp.einsum(
        "nhbc,nbhe->nche", weights_low[..., :BLOCK], grad_mixed, preferred_element_type=jnp.float32
    )
    grad_key_sorted = (
        jnp.einsum("nhbc,nbhd->nchd", grad_s_sorted, query, preferred_element_type=jnp.float32)
        * scale
    )
    grad_value_sorted = jnp.einsum(
        "nhbc,nbhe->nche", weights_low[..., BLOCK:], grad_mixed, preferred_element_type=jnp.float32
    )
    grad_sorted = jnp.concatenate([grad_key_sorted, grad_value_sorted], axis=-1).astype(
        jnp.bfloat16
    )
    grad_sorting = jnp.einsum(
        "nbhe,mbhe->hnm", grad_sorted, context, preferred_element_type=jnp.float32
    )
    grad_context = jnp.einsum(
        "hnm,nbhe->mbhe", sorting_low, grad_sorted, preferred_element_type=jnp.float32
    )
    grad_around, grad_sort = sort_back(grad_sorting)
    later_part = shifted_2(grad_context[:attend_range].astype(jnp.bfloat16), "blk", -1).astype(
        jnp.float32
    )
    grad_keyval = grad_context[attend_range:] + jnp.concatenate(
        [grad_key_local, grad_value_local], axis=-1
    )
    grad_keyval = grad_keyval + jnp.pad(
        later_part, ((document_span_blocks - attend_range, 0), (0, 0), (0, 0), (0, 0))
    )
    rim_back = shifted_2(grad_around[:attend_range], "blk", -1)
    grad_means = grad_around[attend_range:]
    grad_means = grad_means + jnp.pad(
        rim_back, ((document_span_blocks - attend_range, 0), (0, 0), (0, 0))
    )
    grad_query = grad_query + grad_means[:, None, :, :HEAD_DIM] / BLOCK
    grad_key = grad_keyval[..., :HEAD_DIM] + grad_means[:, None, :, HEAD_DIM:] / BLOCK
    grad_blocks = jnp.concatenate(
        [grad_query, grad_key, grad_keyval[..., HEAD_DIM:]], axis=-1
    ).astype(jnp.bfloat16)
    grad_qkv = lax.all_to_all(
        grad_blocks.reshape(span_rows, local_heads, 3 * HEAD_DIM),
        "head",
        split_axis=0,
        concat_axis=1,
        tiled=True,
    )
    grad_qkv = grad_qkv.reshape(tok_rows, 3 * D)
    grad_wqkv = jnp.einsum("td,te->de", normed, grad_qkv, preferred_element_type=jnp.float32)
    grad_normed = jnp.einsum("te,de->td", grad_qkv, weight_qkv, preferred_element_type=jnp.float32)
    grad_resid_norm, grad_gain_one = norm_one_back(grad_normed)
    input_grad = grad_middle + grad_resid_norm

    def spread_out(vector):
        return vector.reshape(head_count, cycle_count, -1)

    grad_sort_rows = grad_sort.reshape(local_heads * HEAD_DIM, HEAD_DIM)
    part = (
        lax.psum_scatter(
            grad_wqkv.astype(jnp.bfloat16), "head", scatter_dimension=0, tiled=True
        ).astype(jnp.float32),
        lax.psum_scatter(
            grad_out.astype(jnp.bfloat16), "head", scatter_dimension=0, tiled=True
        ).astype(jnp.float32),
        lax.psum_scatter(
            grad_in.astype(jnp.bfloat16), "head", scatter_dimension=0, tiled=True
        ).astype(jnp.float32),
        lax.psum_scatter(
            grad_down.astype(jnp.bfloat16), "head", scatter_dimension=0, tiled=True
        ).astype(jnp.float32),
        lax.psum_scatter(
            spread_out(grad_gain_one).astype(jnp.bfloat16), "head", scatter_dimension=0, tiled=True
        ).astype(jnp.float32),
        lax.psum_scatter(
            spread_out(grad_bias_out).astype(jnp.bfloat16), "head", scatter_dimension=0, tiled=True
        ).astype(jnp.float32),
        lax.psum_scatter(
            spread_out(grad_gain_two).astype(jnp.bfloat16), "head", scatter_dimension=0, tiled=True
        ).astype(jnp.float32),
        lax.psum_scatter(
            spread_out(grad_bias_in).astype(jnp.bfloat16), "head", scatter_dimension=0, tiled=True
        ).astype(jnp.float32),
        lax.psum_scatter(
            spread_out(grad_bias_down).astype(jnp.bfloat16), "head", scatter_dimension=0, tiled=True
        ).astype(jnp.float32),
    )
    summed = (
        lax.psum_scatter(
            part[0].astype(jnp.bfloat16), "blk", scatter_dimension=1, tiled=True
        ).astype(jnp.float32),
        lax.psum_scatter(
            part[1].astype(jnp.bfloat16), "blk", scatter_dimension=1, tiled=True
        ).astype(jnp.float32),
        lax.psum_scatter(
            part[2].astype(jnp.bfloat16), "blk", scatter_dimension=1, tiled=True
        ).astype(jnp.float32),
        lax.psum_scatter(
            part[3].astype(jnp.bfloat16), "blk", scatter_dimension=1, tiled=True
        ).astype(jnp.float32),
        lax.psum_scatter(
            part[4].astype(jnp.bfloat16), "blk", scatter_dimension=1, tiled=True
        ).astype(jnp.float32),
        lax.psum_scatter(
            part[5].astype(jnp.bfloat16), "blk", scatter_dimension=1, tiled=True
        ).astype(jnp.float32),
        lax.psum_scatter(
            part[6].astype(jnp.bfloat16), "blk", scatter_dimension=1, tiled=True
        ).astype(jnp.float32),
        lax.psum_scatter(
            part[7].astype(jnp.bfloat16), "blk", scatter_dimension=1, tiled=True
        ).astype(jnp.float32),
        lax.psum_scatter(
            part[8].astype(jnp.bfloat16), "blk", scatter_dimension=1, tiled=True
        ).astype(jnp.float32),
        lax.psum_scatter(
            grad_sort_rows.astype(jnp.bfloat16), "blk", scatter_dimension=1, tiled=True
        ).astype(jnp.float32),
    )
    return (
        output.astype(jnp.bfloat16)[None],
        input_grad[None],
        summed[4].reshape(-1),
        summed[0],
        summed[1],
        summed[5].reshape(-1),
        summed[6].reshape(-1),
        summed[2],
        summed[7].reshape(-1),
        summed[3],
        summed[8].reshape(-1),
        summed[9],
    )


def solution(mesh):
    return jax.shard_map(
        per_device,
        mesh=mesh,
        in_specs=(
            P("blk", "head", None),
            P("blk", "head", None),
            P(),
            P(("head", "blk")),
            P("head", "blk"),
            P("head", "blk"),
            P(("head", "blk")),
            P(("head", "blk")),
            P("head", "blk"),
            P(("head", "blk")),
            P("head", "blk"),
            P(("head", "blk")),
            P("head", "blk"),
        ),
        out_specs=(
            P("blk", "head", None),
            P("blk", "head", None),
            P(("head", "blk")),
            P("head", "blk"),
            P("head", "blk"),
            P(("head", "blk")),
            P(("head", "blk")),
            P("head", "blk"),
            P(("head", "blk")),
            P("head", "blk"),
            P(("head", "blk")),
            P("head", "blk"),
        ),
        check_vma=False,
    )
```

profile of v0, /device:TPU:12, one launch (start us, length us, event | category | flops | bytes accessed | tf_op | source)
XLA Modules:
  0.0 875.5 jit_solution(3795746721890230422)
XLA Ops:
  7.2 16.0 %all_gather.59 = bf16[128,1536]{0,1:T(8,128)(2,1)} all-gather(bf16[128,192]{0,1:T(8,128)(2,1)} %param.17), channel_id=1, replica_groups=mesh['head'=4,'blk'=8] {'blk'}, dimensions={1}, use_global_device_ids=true | all-gather | bytes 442368 | tf_op jit(solution)/shard_map/all_gather | solution.py:97
  29.3 13.4 %all-reduce.22 = (bf16[128]{0:T(256)(128)(2,1)S(1)}, bf16[128]{0:T(256)(128)(2,1)S(1)}, bf16[128]{0:T(256)(128)(2,1)S(1)}, bf16[512]{0:T(512)(128)(2,1)S(1)}) all-reduce(bf16[128]{0:T(256)(128)(2,1)S(1)} %dynamic-update-slice, bf16[128]{0:T(256)(128)(2,1)S(1)} %dynamic-update-slice.1, ...), channel_id=2, replica_groups=mesh['head'=4,'blk'=8] {'blk'}, use_global_device_ids=true, to_apply=%add.5 | all-reduce | flops 896 | bytes 3584
  66.8 15.8 %all_gather.68 = bf16[128,2048]{1,0:T(8,128)(2,1)} all-gather(bf16[128,256]{1,0:T(8,128)(2,1)S(1)} %copy-done.109), channel_id=1, replica_groups=mesh['head'=4,'blk'=8] {'blk'}, dimensions={1}, use_global_device_ids=true | all-gather | bytes 589824 | tf_op jit(solution)/shard_map/all_gather | solution.py:99
  82.7 12.8 %all_gather.61 = bf16[128,64]{0,1:T(8,128)(2,1)S(1)} all-gather(bf16[128,8]{0,1:T(8,128)(2,1)S(1)} %copy-done.196), channel_id=1, replica_groups=mesh['head'=4,'blk'=8] {'blk'}, dimensions={1}, use_global_device_ids=true | all-gather | bytes 18432 | tf_op jit(solution)/shard_map/all_gather | solution.py:101
  96.6 28.6 %all-to-all-done = bf16[1536,8,192]{0,2,1:T(8,128)(2,1)} async-done(((bf16[1536,8,192]{0,2,1:T(8,128)(2,1)}), bf16[1536,8,192]{0,2,1:T(8,128)(2,1)}, u32[]{:S(2)}, u32[]{:S(2)}) %all-to-all-start) | async-done | bytes 4718624 | tf_op jit(solution)/shard_map/all_to_all | solution.py:134
  195.4 9.3 %fusion.185 = (f32[192,2,32]{2,1,0:T(2,128)S(1)}, f32[192,2,32,32]{3,2,1,0:T(8,128)}) fusion(bf16[192,32,2,64]{3,0,1,2:T(8,128)(2,1)S(1)} %get-tuple-element.182, bf16[192,32,2,64]{3,1,0,2:T(8,128)(2,1)S(1)} %copy-done.14, pred[192]{0:T(512)(128)(4,1)S(1)} %get-tuple-element.186), kind=kOutput, calls=%fused_computation.484 | convolution fusion | flops 51499008 | bytes 4767936 | tf_op jit(solution)/shard_map/nbhd,nchd->nhbc/dot_general | solution.py:197
  220.0 26.8 %copy.252 = bf16[6144,2,64]{2,1,0:T(2,128)(2,1)} copy(bf16[6144,2,64]{2,0,1:T(8,128)(2,1)S(1)} %bitcast.193) | data formatting | bytes 3145728 | tf_op jit(solution)/shard_map/reshape | solution.py:220
  256.9 14.4 %all_gather.72 = bf16[512,512]{0,1:T(8,128)(2,1)} all-gather(bf16[512,64]{0,1:T(8,128)(2,1)S(1)} %copy-done.110), channel_id=1, replica_groups=mesh['head'=4,'blk'=8] {'blk'}, dimensions={1}, use_global_device_ids=true | all-gather | bytes 589824 | tf_op jit(solution)/shard_map/all_gather | solution.py:100
  296.7 14.5 %all_gather.62 = bf16[128,512]{0,1:T(8,128)(2,1)S(1)} all-gather(bf16[128,64]{0,1:T(8,128)(2,1)S(1)} %copy-done.195), channel_id=1, replica_groups=mesh['head'=4,'blk'=8] {'blk'}, dimensions={1}, use_global_device_ids=true | all-gather | bytes 147456 | tf_op jit(solution)/shard_map/all_gather | solution.py:98
  311.2 10.7 %all_gather.63 = bf16[512,512]{0,1:T(8,128)(2,1)} all-gather(bf16[128,512]{0,1:T(8,128)(2,1)S(1)} %all_gather.62), channel_id=1, replica_groups=mesh['head'=4,'blk'=8] {'head'}, dimensions={0}, use_global_device_ids=true | all-gather | bytes 655360 | tf_op jit(solution)/shard_map/all_gather | solution.py:110
  340.8 12.9 %multiply_convert_fusion = (bf16[1536,2048]{1,0:T(8,128)(2,1)}, f32[1536,2048]{1,0:T(8,128)}) fusion(f32[2048]{0:T(1024)S(1)} %reshape.1947, bf16[512,2048]{1,0:T(8,128)(2,1)} %all-gather.11.cloned.1.call-done, f32[1536,512]{0,1:T(8,128)} %copy-done.23, f32[512]{0:T(512)S(1)} %reshape.1946, f32[1536]{0:T(1024)S(1)} %fusion.150, ...), kind=kOutput, calls=%fused_computation.10 | convolution fusion | flops 3255828480 | bytes 24139776 | tf_op jit(solution)/shard_map/dot_general | solution.py:230
  353.7 14.0 %fusion.187 = (bf16[2048]{0:T(1024)(128)(2,1)S(1)}, bf16[1536,2048]{1,0:T(8,128)(2,1)S(1)}) fusion(f32[1536,2048]{1,0:T(8,128)} %get-tuple-element.198, f32[2048]{0:T(1024)S(1)} %reshape.1947, bf16[2048,512]{0,1:T(8,128)(2,1)} %all-gather.13.cloned.1.call-done, bf16[1,1536,512]{2,1,0:T(8,128)(2,1)S(1)} %copy-done.28), kind=kOutput, calls=%fused_computation.486 | convolution fusion | flops 3290429440 | bytes 22556672 | tf_op jit(solution)/shard_map/td,fd->tf/dot_general | solution.py:238
  402.0 11.8 %all-to-all-done.2 = bf16[1536,8,64]{0,2,1:T(8,128)(2,1)} async-done(((bf16[1536,8,64]{0,2,1:T(8,128)(2,1)}), bf16[1536,8,64]{0,2,1:T(8,128)(2,1)}, u32[]{:S(2)}, u32[]{:S(2)}) %all-to-all-start.2) | async-done | bytes 1572896 | tf_op jit(solution)/shard_map/all_to_all | solution.py:253
  423.5 69.7 %multiply_convert_fusion.2 = bf16[192,2,32,64]{3,2,1,0:T(8,128)(2,1)} fusion(f32[192,2,32,64]{3,2,1,0:T(8,128)S(1)} %bitcast.189, f32[192,2,32]{2,1,0:T(2,128)S(1)} %bitcast.205, f32[192,2,32,32]{3,2,1,0:T(8,128)S(1)} %fusion.59, f32[192,2,32,32]{3,2,1,0:T(8,128)S(1)} %fusion.52), kind=kOutput, calls=%fused_computation.23 | output fusion | flops 6303807 | bytes 7913472 | tf_op jit(solution)/shard_map/sub | solution.py:268
  493.2 9.3 %fusion.38 = f32[192,2,64,32]{2,3,1,0:T(8,128)} fusion(bf16[192,2,32,64]{3,2,1,0:T(8,128)(2,1)} %multiply_convert_fusion.2, bf16[192,32,2,64]{3,0,1,2:T(8,128)(2,1)} %copy-done.27), kind=kOutput, calls=%fused_computation.78 | convolution fusion | flops 50331648 | bytes 6291456 | tf_op jit(solution)/shard_map/nhbc,nchd->nbhd/dot_general | solution.py:277
  555.0 10.1 %copy.271 = f32[2,32,128,253]{2,1,0,3:T(8,128)} copy(f32[2,32,128,253]{3,2,1,0:T(8,128)} %fusion.55) | data formatting | bytes 16580608 | tf_op jit(solution)/shard_map/hnm,nbhe->mbhe/dot_general | solution.py:301
  598.5 40.4 %copy.278 = bf16[6144,2,192]{2,1,0:T(2,128)(2,1)} copy(bf16[6144,2,192]{2,0,1:T(8,128)(2,1)S(1)} %pad_maximum_fusion.2) | data formatting | bytes 9437184 | tf_op jit(solution)/shard_map/concatenate | solution.py:321
  652.2 22.4 %reduce-scatter.32.cloned.1.call-done = bf16[64,128]{1,0:T(8,128)(2,1)} async-done(((bf16[512,128]{1,0:T(8,128)(2,1)}), bf16[64,128]{1,0:T(8,128)(2,1)}) %reduce-scatter.32.cloned.1.call-update) | async-done | bytes 16400
  676.1 30.4 %reduce-scatter.34.cloned.1.call-done = bf16[64,512]{1,0:T(8,128)(2,1)} async-done(((bf16[512,512]{1,0:T(8,128)(2,1)}), bf16[64,512]{1,0:T(8,128)(2,1)}) %reduce-scatter.34.cloned.1.call-update) | async-done | bytes 65552
  708.2 29.8 %reduce-scatter.26.cloned.1.call-done = bf16[128,256]{1,0:T(8,128)(2,1)} async-done(((bf16[128,2048]{1,0:T(8,128)(2,1)}), bf16[128,256]{1,0:T(8,128)(2,1)}) %reduce-scatter.26.cloned.1.call-update) | async-done | bytes 65552 | tf_op jit(solution)/shard_map/reduce_scatter | solution.py:377
  739.5 16.9 %copy.297 = bf16[4,1536,2,192]{1,0,3,2:T(4,128)(2,1)} copy(bf16[4,1536,2,192]{3,2,1,0:T(2,128)(2,1)} %bitcast.36) | data formatting | bytes 9437184 | tf_op jit(solution)/shard_map/all_to_all | solution.py:324
  774.3 16.5 %all-reduce.23 = (bf16[4,8,16]{2,1,0:T(8,128)(2,1)S(1)}, bf16[4,8,16]{2,1,0:T(8,128)(2,1)S(1)}, bf16[4,8,16]{2,1,0:T(8,128)(2,1)S(1)}, bf16[4,8,64]{2,1,0:T(8,128)(2,1)S(1)}, bf16[4,8,16]{2,1,0:T(8,128)(2,1)S(1)}) all-reduce(bf16[4,8,16]{2,1,0:T(8,128)(2,1)S(1)} %convert_element_type.304, ...), channel_id=7, replica_groups=mesh['head'=4,'blk'=8] {'head'}, use_global_device_ids=true, to_apply=%region_116.117.clone | all-reduce | flops 4096 | bytes 16384
  794.2 25.6 %all-reduce.21 = (bf16[128]{0:T(256)(128)(2,1)S(1)}, bf16[1,8,16]{2,1,0:T(8,128)(2,1)S(1)}, bf16[1,8,16]{2,1,0:T(8,128)(2,1)S(1)}, bf16[1,8,16]{2,1,0:T(8,128)(2...) all-reduce(bf16[128]{0:T(256)(128)(2,1)S(1)} %dynamic-update-slice., ...), channel_id=6, replica_groups=mesh['head'=4,'blk'=8] {'blk'}, use_global_device_ids=true, to_apply=%add.9 | all-reduce | flops 9344 | bytes 37376
  856.7 10.4 %reduce-scatter.30.cloned.1.call-done = bf16[192,128]{1,0:T(8,128)(2,1)} async-done(((bf16[1536,128]{1,0:T(8,128)(2,1)}), bf16[192,128]{1,0:T(8,128)(2,1)}) %reduce-scatter.30.cloned.1.call-update) | async-done | bytes 49168
  (742 shorter events, 363.7 us)
Async XLA Ops:
  7.2 48.0 %all-gather.9.cloned.1.call-start = ((), (), s32[]{:S(2)}) async-start(), calls=%async_computation.12 | async-start | bytes 1966080 | tf_op jit(solution)/shard_map/all_gather | solution.py:109
  52.6 284.7 %copy-start.11 = (bf16[1,1536,512]{1,2,0:T(8,128)(2,1)}, bf16[1,1536,512]{1,2,0:T(8,128)(2,1)S(1)}, u32[]{:S(2)}) copy-start(bf16[1,1536,512]{1,2,0:T(8,128)(2,1)S(1)} %copy.237) | copy-start | bytes 4718596
  61.2 64.0 %all-to-all-start = ((bf16[1536,8,192]{0,2,1:T(8,128)(2,1)}), bf16[1536,8,192]{0,2,1:T(8,128)(2,1)}, u32[]{:S(2)}, u32[]{:S(2)}) async-start(bf16[1536,8,192]{0,2,1:T(8,128)(2,1)} %bitcast.199), calls=%async_computation | async-start | bytes 9437184 | tf_op jit(solution)/shard_map/all_to_all | solution.py:134
  66.8 274.0 %all-gather.11.cloned.1.call-start = ((), (), s32[]{:S(2)}) async-start(), calls=%async_computation.13 | async-start | bytes 2621440 | tf_op jit(solution)/shard_map/all_gather | solution.py:111
  96.2 92.3 %copy-start.66 = (pred[253]{0:T(512)(128)(4,1)}, pred[253]{0:T(512)(128)(4,1)S(1)}, u32[]{:S(2)}) copy-start(pred[253]{0:T(512)(128)(4,1)S(1)} %get-tuple-element.136) | copy-start | bytes 763
  96.3 93.3 %copy-start.68 = (pred[253]{0:T(512)(128)(4,1)}, pred[253]{0:T(512)(128)(4,1)S(1)}, u32[]{:S(2)}) copy-start(pred[253]{0:T(512)(128)(4,1)S(1)} %get-tuple-element.137) | copy-start | bytes 763
  96.4 93.1 %copy-start.4 = (pred[253,253]{1,0:T(8,128)(4,1)}, pred[253,253]{1,0:T(8,128)(4,1)S(1)}, u32[]{:S(2)}) copy-start(pred[253,253]{1,0:T(8,128)(4,1)S(1)} %fusion.113) | copy-start | bytes 192031
  96.6 94.2 %copy-start.75 = (pred[192,253]{1,0:T(8,128)(4,1)}, pred[192,253]{1,0:T(8,128)(4,1)S(1)}, u32[]{:S(2)}) copy-start(pred[192,253]{1,0:T(8,128)(4,1)S(1)} %get-tuple-element.185) | copy-start | bytes 145732
  146.0 13.2 %collective-permute-start.1 = (f32[61,2,128]{0,2,1:T(8,128)S(1)}, f32[61,2,128]{0,2,1:T(8,128)S(1)}, u32[]{:S(2)}, u32[]{:S(2)}) collective-permute-start(f32[61,2,128]{0,2,1:T(8,128)S(1)} %pad_maximum_fusion.12), channel_id=1, source_target_pairs={{0,1},{1,2},{2,3},{3,4},{4,5},{5,6},{6,7},{8,9},{9,10},{10,11},{11... | collective-permute-start | bytes 187400 | tf_op jit(solution)/shard_map/ppermute | solution.py:22
  148.1 41.9 %collective-permute-start = (bf16[61,32,2,128]{3,1,2,0:T(8,128)(2,1)S(1)}, bf16[61,32,2,128]{3,1,2,0:T(8,128)(2,1)S(1)}, u32[]{:S(2)}, u32[]{:S(2)}) collective-permute-start(bf16[61,32,2,128]{3,1,2,0:T(8,128)(2,1)S(1)} %copy.243), channel_id=1, source_target_pairs={{0,1},{1,2},{2,3},{3,4},{4,5},{5,6},{6,7},{8,9},{9,10},{10,11},{11... | collective-permute-start | bytes 2998280 | tf_op jit(solution)/shard_map/ppermute | solution.py:22
  251.9 70.0 %all-to-all-start.1 = ((bf16[4,2,98304]{2,1,0:T(2,128)(2,1)}), bf16[4,2,98304]{2,1,0:T(2,128)(2,1)}, u32[]{:S(2)}, u32[]{:S(2)}) async-start(bf16[4,2,98304]{2,1,0:T(2,128)(2,1)} %reshape.2019), calls=%async_computation.1 | async-start | bytes 3145728 | tf_op jit(solution)/shard_map/all_to_all | solution.py:219
  256.9 96.8 %all-gather.13.cloned.1.call-start = ((), (), s32[]{:S(2)}) async-start(), calls=%async_computation.14 | async-start | bytes 2621440 | tf_op jit(solution)/shard_map/all_gather | solution.py:112
  271.2 373.5 %reduce-scatter.22.cloned.1.call-start = ((), (), s32[]{:S(2)}) async-start(), calls=%async_computation.16 | async-start | bytes 655360 | tf_op jit(solution)/shard_map/reduce_scatter | solution.py:345
  377.7 268.9 %reduce-scatter.28.cloned.1.call-start = ((), (), s32[]{:S(2)}) async-start(), calls=%async_computation.19 | async-start | bytes 2621440 | tf_op jit(solution)/shard_map/reduce_scatter | solution.py:351
  388.8 25.0 %all-to-all-start.2 = ((bf16[1536,8,64]{0,2,1:T(8,128)(2,1)}), bf16[1536,8,64]{0,2,1:T(8,128)(2,1)}, u32[]{:S(2)}, u32[]{:S(2)}) async-start(bf16[1536,8,64]{0,2,1:T(8,128)(2,1)} %bitcast.208), calls=%async_computation.2 | async-start | bytes 3145728 | tf_op jit(solution)/shard_map/all_to_all | solution.py:253
  394.2 254.6 %reduce-scatter.24.cloned.1.call-start = ((), (), s32[]{:S(2)}) async-start(), calls=%async_computation.17 | async-start | bytes 2621440 | tf_op jit(solution)/shard_map/reduce_scatter | solution.py:348
  546.8 25.7 %collective-permute-start.2 = (f32[61,2,128]{0,2,1:T(8,128)}, f32[61,2,128]{0,2,1:T(8,128)}, u32[]{:S(2)}, u32[]{:S(2)}) collective-permute-start(f32[61,2,128]{0,2,1:T(8,128)} %pad_add_fusion), channel_id=1, source_target_pairs={{1,0},{2,1},{3,2},{4,3},{5,4},{6,5},{7,6},{9,8},{10,9},{11,10},{12... | collective-permute-start | bytes 187400 | tf_op jit(solution)/shard_map/ppermute | solution.py:22
  568.0 16.1 %collective-permute-start.3 = (bf16[61,32,2,128]{3,1,2,0:T(8,128)(2,1)}, bf16[61,32,2,128]{3,1,2,0:T(8,128)(2,1)}, u32[]{:S(2)}, u32[]{:S(2)}) collective-permute-start(bf16[61,32,2,128]{3,1,2,0:T(8,128)(2,1)} %slice.183), channel_id=1, source_target_pairs={{1,0},{2,1},{3,2},{4,3},{5,4},{6,5},{7,6},{9,8},{10,9},{11,10},{12... | collective-permute-start | bytes 2998280 | tf_op jit(solution)/shard_map/ppermute | solution.py:22
  639.0 100.5 %all-to-all-start.3 = ((bf16[6144,2,192]{2,1,0:T(2,128)(2,1)}), bf16[6144,2,192]{2,1,0:T(2,128)(2,1)}, u32[]{:S(2)}, u32[]{:S(2)}) async-start(bf16[6144,2,192]{2,1,0:T(2,128)(2,1)} %copy.278), calls=%async_computation.3 | async-start | bytes 12582912 | tf_op jit(solution)/shard_map/all_to_all | solution.py:324
  644.7 29.9 %reduce-scatter.32.cloned.1.call-start = ((), (), s32[]{:S(2)}) async-start(), calls=%async_computation.21 | async-start | bytes 147456
  646.6 59.9 %reduce-scatter.34.cloned.1.call-start = ((), (), s32[]{:S(2)}) async-start(), calls=%async_computation.22 | async-start | bytes 589824
  648.7 89.3 %reduce-scatter.26.cloned.1.call-start = ((), (), s32[]{:S(2)}) async-start(), calls=%async_computation.18 | async-start | bytes 589824 | tf_op jit(solution)/shard_map/reduce_scatter | solution.py:377
  649.5 187.6 %reduce-scatter.20.cloned.1.call-start = ((), (), s32[]{:S(2)}) async-start(), calls=%async_computation.15 | async-start | bytes 1966080 | tf_op jit(solution)/shard_map/reduce_scatter | solution.py:342
  765.9 101.2 %reduce-scatter.30.cloned.1.call-start = ((), (), s32[]{:S(2)}) async-start(), calls=%async_computation.20 | async-start | bytes 442368
  (202 other events, 1221.2 us)
Sparse Core Ops, SparseCore 0:
  23.3 31.8 all-gather.8
  82.8 61.4 all-gather.10
  271.4 36.1 all-gather.12
  377.8 29.3 reduce-scatter.21
  410.3 35.2 reduce-scatter.27
  448.4 35.2 reduce-scatter.23
  648.5 26.0 reduce-scatter.31
  677.4 29.0 reduce-scatter.33
  708.8 29.1 reduce-scatter.25
  766.1 33.5 reduce-scatter.19
  839.1 27.9 reduce-scatter.29
where the time goes:
time: 887 us; the launch traced here: 876 us
  local copies, waits for them, and re-layouts  200 us (23%)
  blocking collectives  179 us (20%)
  other arithmetic  153 us (17%)
  matrix products  143 us (16%)
  waiting for transfers between devices  138 us (16%)
  starting transfers between devices  34.4 us (4%)
  between operations  29.5 us (3%)
    sub x1, other arithmetic, per_device(): grad_weights - jnp.sum(weights * grad_weights, axis=-1, keepdims=True)  69.7 us
    unnamed x14, waiting for transfers between devices  64 us
    unnamed x447, local copies, waits for them, and re-layouts  57.7 us
    unnamed x3, blocking collectives  55.5 us
    concatenate x1, local copies, waits for them, and re-layouts, per_device(): jnp.concatenate([grad_query, grad_key, grad_keyval[..., HEAD_DIM:]], axis...  40.4 us
    reduce_scatter x1, waiting for transfers between devices, per_device(): lax.psum_scatter(part[2].astype(jnp.bfloat16), 'blk', scatter_dimension=1...  29.8 us
    all_to_all x1, waiting for transfers between devices, per_device(): lax.all_to_all(qkv.reshape(tok_rows, HEADS, 3 * HEAD_DIM), 'head', split_...  28.6 us
    reshape x1, local copies, waits for them, and re-layouts, per_device(): mixed.astype(jnp.bfloat16).reshape(span_rows, local_heads, HEAD_DIM)  26.8 us
  transfers between devices with their start and end apart: 19, of which 8 were waited for; matrix products, arithmetic and copies ran while one was open for 48% of the time, Pallas kernels for 0%

commit v1 on v0

v1 whole, which is shorter than its diff:
```python
import functools

import jax
import jax.numpy as jnp
from jax import lax
from jax.experimental import pallas as pl
from jax.experimental.pallas import tpu as pltpu
from jax.sharding import PartitionSpec as P

D = 512
HEADS = 8
HEAD_DIM = 64
FF = 2048
BLOCK = 32
SINK_ITERS = 8
DOC_MOST = 62
LANES = 128
PAIRS = HEADS // 2
HALO = 64
UNROLL = 2
PRECISE = lax.Precision.HIGHEST
EPSILON = 1e-05
NEGATIVE = -1e30
F32 = jnp.float32
BF16 = jnp.bfloat16
NT = (((1,), (1,)), ((), ()))
NN = (((1,), (0,)), ((), ()))
TN = (((0,), (0,)), ((), ()))


def mm(a, b, dims=NN, precision=None):
    return lax.dot_general(a, b, dims, precision=precision, preferred_element_type=F32)


def vmem(limit=56):
    return pltpu.CompilerParams(vmem_limit_bytes=limit * 1024 * 1024)


def sink_mask(docn_ref, docc_ref, window, context):
    first = context
    fold = window - LANES
    lane = lax.broadcasted_iota(jnp.int32, (1, LANES), 1)
    docn = docn_ref[...]
    row = lax.broadcasted_iota(jnp.int32, (window, 1), 0)
    col = jnp.where((row >= first) & (lane < fold), lane + LANES, lane)
    docc = jnp.where(row >= first, docc_ref[1:2, :], docc_ref[0:1, :])
    return (docn == docc) & (docn >= 0) & (col < row)


def fold_pair(top, low, fold, join):
    lane = lax.broadcasted_iota(jnp.int32, (1, LANES), 1)
    both = join(top, low)
    return jnp.where(lane < fold, top, both), jnp.where(lane < fold, low, both)


def sink_weight(w_ref, head):
    pair = w_ref[head // 2]
    lane = lax.broadcasted_iota(jnp.int32, pair.shape, 1)
    zero = jnp.zeros_like(pair)
    if head % 2 == 0:
        return jnp.concatenate([jnp.where(lane < HEAD_DIM, pair, zero), zero], axis=0)
    return jnp.concatenate([zero, jnp.where(lane >= HEAD_DIM, pair, zero)], axis=0)


def sink_logits(queries, keys, weight, context, fold):
    projected = mm(queries, weight, NT, PRECISE)
    keys_two = jnp.concatenate([keys[LANES:], keys[fold:LANES]], axis=0)
    top = mm(projected[:context], keys[:LANES], NT, PRECISE)
    low = mm(projected[context:], keys_two, NT, PRECISE)
    return projected, keys_two, jnp.concatenate([top, low], axis=0)


def row_step(values):
    highest = jnp.max(values, axis=1, keepdims=True)
    alive = highest > 0.5 * NEGATIVE
    highest = jnp.where(alive, highest, 0.0)
    shifted = jnp.exp(values - highest)
    total = jnp.where(alive, jnp.sum(shifted, axis=1, keepdims=True), 1.0)
    return values - (highest + jnp.log(total)), shifted, total


def column_step(values, context, fold):
    top, low = values[:context], values[context:]
    h1, h2 = fold_pair(
        jnp.max(top, axis=0, keepdims=True),
        jnp.max(low, axis=0, keepdims=True),
        fold,
        jnp.maximum,
    )
    a1, a2 = h1 > 0.5 * NEGATIVE, h2 > 0.5 * NEGATIVE
    h1, h2 = jnp.where(a1, h1, 0.0), jnp.where(a2, h2, 0.0)
    e1, e2 = jnp.exp(top - h1), jnp.exp(low - h2)
    t1, t2 = fold_pair(
        jnp.sum(e1, axis=0, keepdims=True), jnp.sum(e2, axis=0, keepdims=True), fold, jnp.add
    )
    t1, t2 = jnp.where(a1, t1, 1.0), jnp.where(a2, t2, 1.0)
    moved = jnp.concatenate([top - (h1 + jnp.log(t1)), low - (h2 + jnp.log(t2))], axis=0)
    return moved, (e1, e2), (t1, t2)


def sink_start(q_ref, k_ref, w_ref, docn_ref, docc_ref, vals, proj, context):
    window = q_ref.shape[0]
    fold = window - LANES
    permitted = sink_mask(docn_ref, docc_ref, window, context)
    for head in range(HEADS):
        lanes = slice(head // 2 * LANES, (head // 2 + 1) * LANES)
        projected, _, logits = sink_logits(
            q_ref[:, lanes], k_ref[:, lanes], sink_weight(w_ref, head), context, fold
        )
        vals[head] = jnp.where(permitted, logits, NEGATIVE)
        if proj is not None:
            proj[head] = projected


def sink_forward_kernel(own, context, q_ref, k_ref, w_ref, docn_ref, docc_ref, plan_ref, vals):
    fold = q_ref.shape[0] - LANES
    sink_start(q_ref, k_ref, w_ref, docn_ref, docc_ref, vals, None, context)

    def step(_, carry):
        for head in range(HEADS):
            moved, _, _ = row_step(vals[head])
            moved, _, _ = column_step(moved, context, fold)
            vals[head] = moved
        return carry

    lax.fori_loop(0, SINK_ITERS, step, 0)
    for head in range(HEADS):
        plan_ref[head] = jnp.exp(vals[head, context - own : context, :]).astype(BF16)


def sink_backward_kernel(
    own, context, q_ref, k_ref, w_ref, docn_ref, docc_ref, gp_ref, gq_ref, gk_ref, gw_ref,
    vals, proj, kept,
):
    window = q_ref.shape[0]
    fold = window - LANES
    sink_start(q_ref, k_ref, w_ref, docn_ref, docc_ref, vals, proj, context)

    def step(at, carry):
        for head in range(HEADS):
            moved, shifted, total = row_step(vals[head])
            kept[2 * at, head] = shifted * (1.0 / total)
            moved, (e1, e2), (t1, t2) = column_step(moved, context, fold)
            kept[2 * at + 1, head, :context, :] = e1 * (1.0 / t1)
            kept[2 * at + 1, head, context:, :] = e2 * (1.0 / t2)
            vals[head] = moved
        return carry

    lax.fori_loop(0, SINK_ITERS, step, 0)
    for head in range(HEADS):
        vals[head] = jnp.concatenate(
            [
                jnp.zeros((context - own, LANES), F32),
                gp_ref[head] * kept[2 * SINK_ITERS - 1, head, context - own : context, :],
                jnp.zeros((window - context, LANES), F32),
            ],
            axis=0,
        )

    def back(turn, carry):
        at = SINK_ITERS - 1 - turn
        for head in range(HEADS):
            g1, g2 = vals[head, :context, :], vals[head, context:, :]
            s1, s2 = fold_pair(
                jnp.sum(g1, axis=0, keepdims=True),
                jnp.sum(g2, axis=0, keepdims=True),
                fold,
                jnp.add,
            )
            grad = jnp.concatenate(
                [
                    g1 - kept[2 * at + 1, head, :context, :] * s1,
                    g2 - kept[2 * at + 1, head, context:, :] * s2,
                ],
                axis=0,
            )
            vals[head] = grad - kept[2 * at, head] * jnp.sum(grad, axis=1, keepdims=True)
        return carry

    lax.fori_loop(0, SINK_ITERS, back, 0)
    for pair in range(PAIRS):
        lanes = slice(pair * LANES, (pair + 1) * LANES)
        queries, keys = q_ref[:, lanes], k_ref[:, lanes]
        keys_two = jnp.concatenate([keys[LANES:], keys[fold:LANES]], axis=0)
        gq_total = jnp.zeros((window, LANES), F32)
        gk_total = jnp.zeros((window, LANES), F32)
        turned = []
        for head in (2 * pair, 2 * pair + 1):
            g1, g2 = vals[head, :context, :], vals[head, context:, :]
            against = jnp.concatenate(
                [mm(g1, keys[:LANES], NN, PRECISE), mm(g2, keys_two, NN, PRECISE)], axis=0
            )
            gq_total = gq_total + mm(against, sink_weight(w_ref, head), NN, PRECISE)
            u1 = mm(g1, proj[head, :context, :], TN, PRECISE)
            u2 = mm(g2, proj[head, context:, :], TN, PRECISE)
            gk_total = gk_total + jnp.concatenate(
                [u1[:fold], u1[fold:] + u2[fold:], u2[:fold]], axis=0
            )
            turned.append(mm(against, queries, TN, PRECISE))
        half = lax.broadcasted_iota(jnp.int32, (HEAD_DIM, LANES), 1) < HEAD_DIM
        gw_ref[pair] = jnp.where(half, turned[0][:HEAD_DIM], turned[1][HEAD_DIM:])
        gq_ref[:, lanes] = gq_total
        gk_ref[:, lanes] = gk_total


def sink_forward(qmean, kmean, weight, docn, docc, own, context):
    window = qmean.shape[0]
    return pl.pallas_call(
        functools.partial(sink_forward_kernel, own, context),
        out_shape=jax.ShapeDtypeStruct((HEADS, own, LANES), BF16),
        scratch_shapes=[pltpu.VMEM((HEADS, window, LANES), F32)],
        compiler_params=vmem(),
        name="sink_forward",
    )(qmean, kmean, weight, docn, docc)


def sink_backward(qmean, kmean, weight, docn, docc, gplan, own, context):
    window = qmean.shape[0]
    return pl.pallas_call(
        functools.partial(sink_backward_kernel, own, context),
        out_shape=[
            jax.ShapeDtypeStruct((window, D), F32),
            jax.ShapeDtypeStruct((window, D), F32),
            jax.ShapeDtypeStruct((PAIRS, HEAD_DIM, LANES), F32),
        ],
        scratch_shapes=[
            pltpu.VMEM((HEADS, window, LANES), F32),
            pltpu.VMEM((HEADS, window, LANES), F32),
            pltpu.VMEM((2 * SINK_ITERS, HEADS, window, LANES), F32),
        ],
        compiler_params=vmem(),
        name="sink_backward",
    )(qmean, kmean, weight, docn, docc, gplan)


def normalise(values):
    centre = values - jnp.mean(values, axis=-1, keepdims=True)
    spread = jnp.mean(centre * centre, axis=-1, keepdims=True)
    return centre * lax.rsqrt(spread + EPSILON)


def context_kernel(halo_blocks, x_ref, gain_ref, w_ref, kvx_ref, nh_ref):
    blocks = x_ref.shape[0]
    normed = normalise(x_ref[...].astype(F32)) * gain_ref[...].reshape(1, 1, D)
    normed = normed.astype(BF16).reshape(blocks * 8, D)
    row = lax.broadcasted_iota(jnp.int32, (LANES, LANES), 0)
    lane = lax.broadcasted_iota(jnp.int32, (LANES, LANES), 1)
    turn = (lane == (row % 16) * 8 + row // 16).astype(F32).astype(BF16)
    turned = [
        mm(turn, normed[i * LANES : (i + 1) * LANES]).astype(BF16) for i in range(blocks // 16)
    ]
    for b in range(8):
        rows = jnp.concatenate([part[b * 16 : (b + 1) * 16] for part in turned], axis=0)
        nh_ref[b] = rows[:halo_blocks]
        out = mm(rows, w_ref[...], NT).astype(BF16)
        for head in range(HEADS):
            kvx_ref[head, :, b * LANES : (b + 1) * LANES] = out[
                :, head * LANES : (head + 1) * LANES
            ]


def context_project(x_context, gain, w_kv, halo_blocks):
    blocks = x_context.shape[0]
    return pl.pallas_call(
        functools.partial(context_kernel, halo_blocks),
        grid=(BLOCK // 8,),
        in_specs=[
            pl.BlockSpec((blocks, 8, D), lambda i: (0, i, 0)),
            pl.BlockSpec((1, D), lambda i: (0, 0)),
            pl.BlockSpec((2 * D, D), lambda i: (0, 0)),
        ],
        out_specs=[
            pl.BlockSpec((HEADS, blocks, 8 * LANES), lambda i: (0, 0, i)),
            pl.BlockSpec((8, halo_blocks, D), lambda i: (i, 0, 0)),
        ],
        out_shape=[
            jax.ShapeDtypeStruct((HEADS, blocks, BLOCK * LANES), BF16),
            jax.ShapeDtypeStruct((BLOCK, halo_blocks, D), BF16),
        ],
        compiler_params=vmem(),
        name="context_project",
    )(x_context, gain, w_kv)


def compact(values, lane_block):
    out = values[:BLOCK]
    for j in range(1, 4):
        out = jnp.where(lane_block == j, values[j * BLOCK : (j + 1) * BLOCK], out)
    return out


def spread(values, lane_block):
    zero = jnp.zeros_like(values)
    return jnp.concatenate([jnp.where(lane_block == j, values, zero) for j in range(4)], axis=0)


def softmax_pair(local, chosen, live):
    lane = lax.broadcasted_iota(jnp.int32, (BLOCK, LANES), 1)
    row = lax.broadcasted_iota(jnp.int32, (BLOCK, LANES), 0)
    local = jnp.where(row <= lax.rem(lane, BLOCK), local, NEGATIVE)
    chosen = jnp.where(live, chosen, NEGATIVE)
    highest = jnp.maximum(
        jnp.max(local, axis=0, keepdims=True), jnp.max(chosen, axis=0, keepdims=True)
    )
    el, es = jnp.exp(local - highest), jnp.exp(chosen - highest)
    total = jnp.sum(el, axis=0, keepdims=True) + jnp.sum(es, axis=0, keepdims=True)
    inverse = 1.0 / total
    return el * inverse, es * inverse


def half_mask(first):
    lane = lax.broadcasted_iota(jnp.int32, (LANES, LANES), 1)
    return (lane < HEAD_DIM) if first else (lane >= HEAD_DIM)


def attend_kernel(q_ref, kv_ref, kvx_ref, plan_ref, live_ref, att_ref, skv_ref, even_ref, odd_ref):
    own = plan_ref.shape[1]
    blocks = kvx_ref.shape[1]
    held = (even_ref, odd_ref)
    for e in range(2):
        plan = plan_ref[e][:, :blocks]
        for chunk in range(4):
            out = mm(plan, kvx_ref[e, :, chunk * 8 * LANES : (chunk + 1) * 8 * LANES])
            for b in range(8):
                at = (chunk * 8 + b) * (own + 1)
                held[e][at : at + own, :] = out[:, b * LANES : (b + 1) * LANES]
    lane_block = lax.broadcasted_iota(jnp.int32, (BLOCK, LANES), 1) // BLOCK
    lane_half = [half_mask(True), half_mask(False)]

    def group(g, carry):
        start = pl.multiple_of(g * LANES, LANES)
        live = live_ref[pl.ds(g, 1), :] > 0.0
        q = q_ref[pl.ds(start, LANES), :] * 0.125
        outs = []
        for e in range(2):
            local = kv_ref[pl.ds(start, LANES), e * LANES : (e + 1) * LANES]
            chosen = jnp.concatenate(
                [held[e][pl.ds(4 * g + i, BLOCK, stride=own + 1), :] for i in range(4)], axis=0
            ).astype(BF16)
            skv_ref[pl.ds(start, LANES), e * LANES : (e + 1) * LANES] = chosen
            both = jnp.concatenate([local, chosen], axis=0)
            qm = jnp.where(lane_half[e], q, jnp.zeros_like(q))
            scores = mm(both, qm, NT)
            wl, ws = softmax_pair(
                compact(scores[:LANES], lane_block), compact(scores[LANES:], lane_block), live
            )
            weights = jnp.concatenate(
                [spread(wl, lane_block), spread(ws, lane_block)], axis=0
            ).astype(BF16)
            turned = both.T
            values = turned[HEAD_DIM:] if e == 0 else turned[:HEAD_DIM]
            outs.append(mm(values, weights))
        att_ref[pl.ds(start, LANES), :] = jnp.concatenate(outs, axis=0).T.astype(BF16)
        return carry

    lax.fori_loop(0, own // 4, group, 0, unroll=UNROLL)


def attend(q, kv, kvx, plan, live):
    tok, own, blocks = q.shape[0], plan.shape[1], kvx.shape[1]
    return pl.pallas_call(
        attend_kernel,
        grid=(PAIRS,),
        in_specs=[
            pl.BlockSpec((tok, LANES), lambda j: (0, j)),
            pl.BlockSpec((tok, 2 * LANES), lambda j: (0, j)),
            pl.BlockSpec((2, blocks, BLOCK * LANES), lambda j: (j, 0, 0)),
            pl.BlockSpec((2, own, LANES), lambda j: (j, 0, 0)),
            pl.BlockSpec((tok // LANES, LANES), lambda j: (0, 0)),
        ],
        out_specs=[
            pl.BlockSpec((tok, LANES), lambda j: (0, j)),
            pl.BlockSpec((tok, 2 * LANES), lambda j: (0, j)),
        ],
        out_shape=[
            jax.ShapeDtypeStruct((tok, D), BF16),
            jax.ShapeDtypeStruct((tok, 2 * D), BF16),
        ],
        scratch_shapes=[pltpu.VMEM((BLOCK * (own + 1), LANES), F32)] * 2,
        compiler_params=vmem(),
        name="attend",
    )(q, kv, kvx, plan, live)


def attend_back_kernel(
    q_ref, kv_ref, skv_ref, go_ref, kvx_ref, plan_ref, live_ref,
    gq_ref, gkv_ref, gh_ref, gp_ref, even_ref, odd_ref, leven_ref, lodd_ref,
):
    own = plan_ref.shape[1]
    blocks = kvx_ref.shape[1]
    halo = blocks - own
    held = (even_ref, odd_ref)
    lheld = (leven_ref, lodd_ref)
    lane_block = lax.broadcasted_iota(jnp.int32, (BLOCK, LANES), 1) // BLOCK
    lane_half = [half_mask(True), half_mask(False)]

    def group(g, carry):
        start = pl.multiple_of(g * LANES, LANES)
        live = live_ref[pl.ds(g, 1), :] > 0.0
        q = q_ref[pl.ds(start, LANES), :] * 0.125
        go = go_ref[pl.ds(start, LANES), :]
        go = jnp.concatenate([go[:, HEAD_DIM:], go[:, :HEAD_DIM]], axis=1)
        outs = []
        for e in range(2):
            local = kv_ref[pl.ds(start, LANES), e * LANES : (e + 1) * LANES]
            chosen = skv_ref[pl.ds(start, LANES), e * LANES : (e + 1) * LANES]
            both = jnp.concatenate([local, chosen], axis=0)
            qm = jnp.where(lane_half[e], q, jnp.zeros_like(q))
            gm = jnp.where(lane_half[1 - e], go, jnp.zeros_like(go))
            right = jnp.concatenate([qm, gm], axis=0)
            scores = mm(both, right, NT)
            wl, ws = softmax_pair(
                compact(scores[:LANES, :LANES], lane_block),
                compact(scores[LANES:, :LANES], lane_block),
                live,
            )
            dl = compact(scores[:LANES, LANES:], lane_block)
            ds = compact(scores[LANES:, LANES:], lane_block)
            inner = jnp.sum(wl * dl, axis=0, keepdims=True) + jnp.sum(
                ws * ds, axis=0, keepdims=True
            )
            gl, gs = wl * (dl - inner), ws * (ds - inner)
            weights = jnp.concatenate(
                [spread(wl, lane_block), spread(ws, lane_block)], axis=0
            ).astype(BF16)
            gscore = jnp.concatenate(
                [spread(gl, lane_block), spread(gs, lane_block)], axis=0
            ).astype(BF16)
            gboth = mm(jnp.concatenate([gscore, weights], axis=1), right)
            lheld[e][pl.ds(start, LANES), :] = gboth[:LANES]
            gchosen = gboth[LANES:]
            for i in range(4):
                held[e][pl.ds(4 * g + i, BLOCK, stride=own + 1), :] = gchosen[
                    i * BLOCK : (i + 1) * BLOCK
                ]
            turned = both.T
            keys = turned[:HEAD_DIM] if e == 0 else turned[HEAD_DIM:]
            outs.append(mm(keys, gscore))
        gq_ref[pl.ds(start, LANES), :] = (jnp.concatenate(outs, axis=0).T * 0.125).astype(BF16)
        return carry

    lax.fori_loop(0, own // 4, group, 0, unroll=UNROLL)
    for e in range(2):
        plan = plan_ref[e][:, :blocks]
        gplan = jnp.zeros((own, blocks), F32)
        for chunk in range(4):
            lanes = slice(chunk * 8 * LANES, (chunk + 1) * 8 * LANES)
            grads = jnp.concatenate(
                [
                    held[e][(chunk * 8 + b) * (own + 1) : (chunk * 8 + b) * (own + 1) + own, :]
                    for b in range(8)
                ],
                axis=1,
            ).astype(BF16)
            gplan = gplan + mm(grads, kvx_ref[e, :, lanes], NT)
            gcontext = mm(plan, grads, TN)
            gh_ref[e, :, lanes] = gcontext[:halo].astype(BF16)
            for b in range(8):
                at = (chunk * 8 + b) * (own + 1)
                held[e][at : at + own, :] = gcontext[halo:, b * LANES : (b + 1) * LANES]
        gp_ref[e] = jnp.concatenate([gplan, jnp.zeros((own, LANES - blocks), F32)], axis=1)

    def finish(g, carry):
        start = pl.multiple_of(g * LANES, LANES)
        for e in range(2):
            rest = jnp.concatenate(
                [held[e][pl.ds(4 * g + i, BLOCK, stride=own + 1), :] for i in range(4)], axis=0
            )
            gkv_ref[pl.ds(start, LANES), e * LANES : (e + 1) * LANES] = (
                rest + lheld[e][pl.ds(start, LANES), :]
            ).astype(BF16)
        return carry

    lax.fori_loop(0, own // 4, finish, 0)


def attend_back(q, kv, skv, go, kvx, plan, live):
    tok, own, blocks = q.shape[0], plan.shape[1], kvx.shape[1]
    halo = blocks - own
    return pl.pallas_call(
        attend_back_kernel,
        grid=(PAIRS,),
        in_specs=[
            pl.BlockSpec((tok, LANES), lambda j: (0, j)),
            pl.BlockSpec((tok, 2 * LANES), lambda j: (0, j)),
            pl.BlockSpec((tok, 2 * LANES), lambda j: (0, j)),
            pl.BlockSpec((tok, LANES), lambda j: (0, j)),
            pl.BlockSpec((2, blocks, BLOCK * LANES), lambda j: (j, 0, 0)),
            pl.BlockSpec((2, own, LANES), lambda j: (j, 0, 0)),
            pl.BlockSpec((tok // LANES, LANES), lambda j: (0, 0)),
        ],
        out_specs=[
            pl.BlockSpec((tok, LANES), lambda j: (0, j)),
            pl.BlockSpec((tok, 2 * LANES), lambda j: (0, j)),
            pl.BlockSpec((2, halo, BLOCK * LANES), lambda j: (j, 0, 0)),
            pl.BlockSpec((2, own, LANES), lambda j: (j, 0, 0)),
        ],
        out_shape=[
            jax.ShapeDtypeStruct((tok, D), BF16),
            jax.ShapeDtypeStruct((tok, 2 * D), BF16),
            jax.ShapeDtypeStruct((HEADS, halo, BLOCK * LANES), BF16),
            jax.ShapeDtypeStruct((HEADS, own, LANES), F32),
        ],
        scratch_shapes=[pltpu.VMEM((BLOCK * (own + 1), LANES), F32)] * 4,
        compiler_params=vmem(),
        name="attend_back",
    )(q, kv, skv, go, kvx, plan, live)


def halo_kernel(gh_ref, nh_ref, w_ref, gn_ref, gw_ref):
    halo = gh_ref.shape[1]

    @pl.when(pl.program_id(0) == 0)
    def _():
        gw_ref[...] = jnp.zeros_like(gw_ref)

    rows = jnp.concatenate(
        [
            jnp.concatenate(
                [gh_ref[head, :, b * LANES : (b + 1) * LANES] for head in range(HEADS)], axis=1
            )
            for b in range(8)
        ],
        axis=0,
    )
    gn_ref[...] = mm(rows, w_ref[...]).astype(BF16).reshape(8, halo, D)
    gw_ref[...] += mm(rows, nh_ref[...].reshape(8 * halo, D), TN)


def halo_back(gh, nh, w_kv):
    halo = gh.shape[1]
    return pl.pallas_call(
        halo_kernel,
        grid=(BLOCK // 8,),
        in_specs=[
            pl.BlockSpec((HEADS, halo, 8 * LANES), lambda i: (0, 0, i)),
            pl.BlockSpec((8, halo, D), lambda i: (i, 0, 0)),
            pl.BlockSpec((2 * D, D), lambda i: (0, 0)),
        ],
        out_specs=[
            pl.BlockSpec((8, halo, D), lambda i: (i, 0, 0)),
            pl.BlockSpec((2 * D, D), lambda i: (0, 0)),
        ],
        out_shape=[
            jax.ShapeDtypeStruct((BLOCK, halo, D), BF16),
            jax.ShapeDtypeStruct((2 * D, D), F32),
        ],
        compiler_params=vmem(),
        name="halo_back",
    )(gh, nh, w_kv)


def project_kernel(x_ref, gain_ref, wq_ref, wkv_ref, n_ref, q_ref, kv_ref, qm_ref, km_ref):
    rows = x_ref.shape[0]
    blocks = rows // BLOCK
    normed = (normalise(x_ref[...].astype(F32)) * gain_ref[...]).astype(BF16)
    n_ref[...] = normed
    q = mm(normed, wq_ref[...], NT).astype(BF16)
    q_ref[...] = q
    kv = mm(normed, wkv_ref[...], NT).astype(BF16)
    kv_ref[...] = kv
    half = lax.broadcasted_iota(jnp.int32, (1, LANES), 1) < HEAD_DIM
    qm_ref[...] = jnp.mean(q.astype(F32).reshape(blocks, BLOCK, D), axis=1)
    for pair in range(PAIRS):
        even = kv[:, 2 * pair * LANES : (2 * pair + 1) * LANES]
        odd = kv[:, (2 * pair + 1) * LANES : (2 * pair + 2) * LANES]
        keys = jnp.where(half, even.astype(F32), odd.astype(F32))
        km_ref[:, pair * LANES : (pair + 1) * LANES] = jnp.mean(
            keys.reshape(blocks, BLOCK, LANES), axis=1
        )


def project(x, gain, wt_q, wt_kv):
    tok = x.shape[0]
    tile = 8 * BLOCK
    return pl.pallas_call(
        project_kernel,
        grid=(tok // tile,),
        in_specs=[
            pl.BlockSpec((tile, D), lambda i: (i, 0)),
            pl.BlockSpec((1, D), lambda i: (0, 0)),
            pl.BlockSpec((D, D), lambda i: (0, 0)),
            pl.BlockSpec((2 * D, D), lambda i: (0, 0)),
        ],
        out_specs=[
            pl.BlockSpec((tile, D), lambda i: (i, 0)),
            pl.BlockSpec((tile, D), lambda i: (i, 0)),
            pl.BlockSpec((tile, 2 * D), lambda i: (i, 0)),
            pl.BlockSpec((8, D), lambda i: (i, 0)),
            pl.BlockSpec((8, D), lambda i: (i, 0)),
        ],
        out_shape=[
            jax.ShapeDtypeStruct((tok, D), BF16),
            jax.ShapeDtypeStruct((tok, D), BF16),
            jax.ShapeDtypeStruct((tok, 2 * D), BF16),
            jax.ShapeDtypeStruct((tok // BLOCK, D), F32),
            jax.ShapeDtypeStruct((tok // BLOCK, D), F32),
        ],
        compiler_params=vmem(),
        name="project",
    )(x, gain, wt_q, wt_kv)


PIECE_ONE = 208
PIECE_TWO = 576
PARTS_TWO = 592


def turn(value):
    return value.astype(F32).T.astype(BF16)


def pack_kernel(wqkv_ref, wsort_ref, vec_ref, win_ref, wdown_ref, wout_ref, one_ref, two_ref):
    one_ref[...] = jnp.concatenate(
        [
            wqkv_ref[...].astype(F32).T,
            wsort_ref[...].astype(F32).T,
            vec_ref[...].astype(F32),
            jnp.zeros((PIECE_ONE - 201, LANES), F32),
        ],
        axis=0,
    ).astype(BF16)
    two_ref[:256, :] = turn(win_ref[...])
    for k in range(4):
        two_ref[256 + k * 64 : 256 + (k + 1) * 64, :] = turn(
            wdown_ref[k * LANES : (k + 1) * LANES, :]
        )
    two_ref[512:, :] = turn(wout_ref[...])


def pack(w_qkv, w_sort, vectors, w_in, w_down, w_out):
    return pl.pallas_call(
        pack_kernel,
        out_shape=[
            jax.ShapeDtypeStruct((PIECE_ONE, LANES), BF16),
            jax.ShapeDtypeStruct((PIECE_TWO, LANES), BF16),
        ],
        compiler_params=vmem(),
        name="pack",
    )(w_qkv, w_sort, vectors, w_in, w_down, w_out)


def each_piece(at_ref, mine_ref, other_ref, visit):
    for core in range(2):

        @pl.when(at_ref[2] == core)
        def _():
            for h in range(4):
                for z in range(4):
                    for c in range(2):
                        source = mine_ref if c == core else other_ref
                        visit(h, z, c, source.at[at_ref[1] ^ z, at_ref[0] ^ h])


def widen(vecs, start, size):
    total = 32 * size
    lane = lax.broadcasted_iota(jnp.int32, (LANES, total), 1)
    row = lax.broadcasted_iota(jnp.int32, (LANES, total), 0)
    pick = (row == start + lax.rem(lane, size)).astype(F32).astype(BF16)
    every = mm(vecs, pick)
    owner = lax.broadcasted_iota(jnp.int32, (32, total), 0)
    lane = lax.broadcasted_iota(jnp.int32, (32, total), 1)
    return jnp.sum(jnp.where(owner == lane // size, every, 0.0), axis=0, keepdims=True)


def assemble_kernel(
    at_ref, mine_ref, other_ref, wq_ref, wkv_ref, ws_ref, g1_ref, bo_ref, g2_ref, bi_ref, bd_ref,
    vecs_ref,
):
    def visit(h, z, c, piece):
        b = 2 * z + c
        lanes = slice(h * LANES, (h + 1) * LANES)
        wq_ref[b * 64 : (b + 1) * 64, lanes] = piece[:64, :]
        base = b * LANES
        wkv_ref[base : base + 64, lanes] = piece[64:128, :] if c == 0 else piece[128:192, :]
        wkv_ref[base + 64 : base + 128, lanes] = piece[128:192, :] if c == 0 else piece[64:128, :]
        tail = piece[192:208, :].astype(F32)
        ws_ref[h, b * 8 : (b + 1) * 8, :] = tail[:8]
        vecs_ref[h * 8 + b : h * 8 + b + 1, :] = tail[8:9]

    each_piece(at_ref, mine_ref, other_ref, visit)
    vecs = vecs_ref[...].astype(BF16)
    g1_ref[...] = widen(vecs, 0, 16)
    bo_ref[...] = widen(vecs, 16, 16)
    g2_ref[...] = widen(vecs, 32, 16)
    bi_ref[...] = widen(vecs, 48, 64)
    bd_ref[...] = widen(vecs, 112, 16)


SMEM = pl.BlockSpec(memory_space=pltpu.SMEM)
VMEM = pl.BlockSpec(memory_space=pltpu.VMEM)


def assemble(at, mine, other):
    row = jax.ShapeDtypeStruct((1, D), F32)
    return pl.pallas_call(
        assemble_kernel,
        in_specs=[SMEM, VMEM, VMEM],
        out_shape=[
            jax.ShapeDtypeStruct((D, D), BF16),
            jax.ShapeDtypeStruct((2 * D, D), BF16),
            jax.ShapeDtypeStruct((PAIRS, HEAD_DIM, LANES), F32),
            row, row, row, jax.ShapeDtypeStruct((1, FF), F32), row,
        ],
        scratch_shapes=[pltpu.VMEM((32, LANES), F32)],
        compiler_params=vmem(),
        name="assemble",
    )(at, mine, other)


GELU_A = 0.7978845608028654
GELU_B = 0.044715


def feed_tile(x, att, g, bo, g2, bi, bd, win, wdown, wout, acc_in, acc_down, acc_out, sums):
    middle = x.astype(F32) + mm(att, wout[...], NT) + bo
    centre = middle - jnp.mean(middle, axis=-1, keepdims=True)
    spread_ = jnp.mean(centre * centre, axis=-1, keepdims=True)
    inverse = lax.rsqrt(spread_ + EPSILON)
    hat = centre * inverse
    normed = (hat * g2).astype(BF16)
    normed_t = normed.T
    g_t = g.T
    out = jnp.zeros(middle.shape, F32)
    u = jnp.zeros(middle.shape, F32)
    cut = 512
    for k in range(FF // cut):
        cols = slice(k * cut, (k + 1) * cut)
        pre = mm(normed, win[cols, :], NT) + bi[:, cols]
        square = pre * pre
        t = jnp.tanh(GELU_A * pre * (1.0 + GELU_B * square))
        half = 0.5 * (1.0 + t)
        hidden = (pre * half).astype(BF16)
        slope = half + (0.5 * GELU_A) * pre * (1.0 - t * t) * (1.0 + (3.0 * GELU_B) * square)
        g_pre = (mm(g, wdown[:, cols], NN) * slope).astype(BF16)
        out = out + mm(hidden, wdown[:, cols], NT)
        u = u + mm(g_pre, win[cols, :], NN)
        acc_in[:, cols] += mm(normed_t, g_pre)
        acc_down[:, cols] += mm(g_t, hidden)
        sums[4:5, cols] += jnp.sum(g_pre.astype(F32), axis=0, keepdims=True)
    gf = g.astype(F32)
    sums[1:2, :D] += jnp.sum(u * hat, axis=0, keepdims=True)
    sums[3:4, :D] += jnp.sum(gf, axis=0, keepdims=True)
    du = u * g2
    inner = jnp.mean(du * hat, axis=-1, keepdims=True)
    g_middle = gf + inverse * (du - jnp.mean(du, axis=-1, keepdims=True) - hat * inner)
    branch = g_middle.astype(BF16)
    sums[0:1, :D] += jnp.sum(branch.astype(F32), axis=0, keepdims=True)
    acc_out[...] += mm(branch.T, att)
    return (middle + out + bd).astype(BF16), g_middle, mm(branch, wout[...], NN).astype(BF16)


def clear(*refs):
    for ref in refs:
        ref[...] = jnp.zeros_like(ref)


def narrow(sums, h, b):
    lane = lax.broadcasted_iota(jnp.int32, (1, LANES), 1)
    owner = h * 8 + b
    row = jnp.zeros((1, LANES), F32)
    for index, start, size in ((0, 16, 16), (1, 32, 16), (4, 48, 64), (3, 112, 16)):
        at = owner * size
        tile = sums[index : index + 1, at // LANES * LANES : at // LANES * LANES + LANES]
        tile = pltpu.roll(jnp.broadcast_to(tile, (8, LANES)), (start - at) % LANES, 1)[:1]
        row = jnp.where((lane >= start) & (lane < start + size), tile, row)
    return row


def feed_fast_kernel(
    at_ref, x_ref, att_ref, g_ref, bo_ref, g2_ref, bi_ref, bd_ref, mine_ref, other_ref,
    out_ref, gm_ref, ga_ref, keep_ref, send_ref,
    win, wdown, wout, acc_in, acc_down, acc_out, sums,
):
    @pl.when(pl.program_id(0) == 0)
    def _():
        def visit(h, z, c, piece):
            b = 2 * z + c
            win[b * 256 : (b + 1) * 256, h * LANES : (h + 1) * LANES] = piece[:256, :]
            for k in range(4):
                lanes = slice(h * 512 + k * LANES, h * 512 + (k + 1) * LANES)
                wdown[b * 64 : (b + 1) * 64, lanes] = piece[256 + k * 64 : 320 + k * 64, :]
            wout[b * 64 : (b + 1) * 64, h * LANES : (h + 1) * LANES] = piece[512:576, :]

        each_piece(at_ref, mine_ref, other_ref, visit)
        clear(acc_in, acc_down, acc_out, sums)

    out_ref[...], gm_ref[...], ga_ref[...] = feed_tile(
        x_ref[...], att_ref[...], g_ref[...], bo_ref[...], g2_ref[...], bi_ref[...], bd_ref[...],
        win, wdown, wout, acc_in, acc_down, acc_out, sums,
    )

    @pl.when(pl.program_id(0) == pl.num_programs(0) - 1)
    def _():
        for core in range(2):

            @pl.when(at_ref[2] == core)
            def _():
                for h in range(4):
                    for z in range(4):
                        for c in range(2):
                            ref = keep_ref if c == core else send_ref
                            b = 2 * z + c
                            for k in range(2):
                                ref[z, h, k * LANES : (k + 1) * LANES, :] = acc_in[
                                    h * LANES : (h + 1) * LANES,
                                    b * 256 + k * LANES : b * 256 + (k + 1) * LANES,
                                ].astype(BF16)
                            for k in range(4):
                                ref[z, h, 256 + k * 64 : 320 + k * 64, :] = acc_down[
                                    b * 64 : (b + 1) * 64,
                                    h * 512 + k * LANES : h * 512 + (k + 1) * LANES,
                                ].astype(BF16)
                            ref[z, h, 512:576, :] = acc_out[
                                b * 64 : (b + 1) * 64, h * LANES : (h + 1) * LANES
                            ].astype(BF16)
                            ref[z, h, 576:592, :] = jnp.broadcast_to(
                                narrow(sums, h, b), (16, LANES)
                            ).astype(BF16)


def once(shape):
    return pl.BlockSpec(shape, lambda *i: (0,) * len(shape), pipeline_mode=pl.Buffered(1))


def feed_fast(at, x, att, g, bo, g2, bi, bd, mine, other):
    tok = x.shape[0]
    tile = 512
    tiled = pl.BlockSpec((tile, D), lambda i: (i, 0))
    parts = (4, 4, PARTS_TWO, LANES)
    return pl.pallas_call(
        feed_fast_kernel,
        grid=(tok // tile,),
        in_specs=[
            SMEM, tiled, tiled, tiled, once((1, D)), once((1, D)), once((1, FF)), once((1, D)),
            once(mine.shape), once(other.shape),
        ],
        out_specs=[tiled, tiled, tiled, once(parts), once(parts)],
        out_shape=[
            jax.ShapeDtypeStruct((tok, D), BF16),
            jax.ShapeDtypeStruct((tok, D), F32),
            jax.ShapeDtypeStruct((tok, D), BF16),
            jax.ShapeDtypeStruct(parts, BF16),
            jax.ShapeDtypeStruct(parts, BF16),
        ],
        scratch_shapes=[
            pltpu.VMEM((FF, D), BF16), pltpu.VMEM((D, FF), BF16), pltpu.VMEM((D, D), BF16),
            pltpu.VMEM((D, FF), F32), pltpu.VMEM((D, FF), F32), pltpu.VMEM((D, D), F32),
            pltpu.VMEM((8, FF), F32),
        ],
        compiler_params=vmem(60),
        name="feed",
    )(at, x, att, g, bo, g2, bi, bd, mine, other)


def feed_slow_kernel(
    x_ref, att_ref, g_ref, bo_ref, g2_ref, bi_ref, bd_ref, win, wdown, wout,
    out_ref, gm_ref, ga_ref, acc_in, acc_down, acc_out, sums,
):
    @pl.when(pl.program_id(0) == 0)
    def _():
        clear(acc_in, acc_down, acc_out, sums)

    out_ref[...], gm_ref[...], ga_ref[...] = feed_tile(
        x_ref[...], att_ref[...], g_ref[...], bo_ref[...], g2_ref[...], bi_ref[...], bd_ref[...],
        win, wdown, wout, acc_in, acc_down, acc_out, sums,
    )


def feed_slow(x, att, g, bo, g2, bi, bd, win, wdown, wout):
    tok = x.shape[0]
    tile = 512
    tiled = pl.BlockSpec((tile, D), lambda i: (i, 0))
    wide, square, rows = (D, FF), (D, D), (8, FF)
    return pl.pallas_call(
        feed_slow_kernel,
        grid=(tok // tile,),
        in_specs=[
            tiled, tiled, tiled, once((1, D)), once((1, D)), once((1, FF)), once((1, D)),
            once((FF, D)), once(wide), once(square),
        ],
        out_specs=[tiled, tiled, tiled, once(wide), once(wide), once(square), once(rows)],
        out_shape=[
            jax.ShapeDtypeStruct((tok, D), BF16),
            jax.ShapeDtypeStruct((tok, D), F32),
            jax.ShapeDtypeStruct((tok, D), BF16),
            jax.ShapeDtypeStruct(wide, F32),
            jax.ShapeDtypeStruct(wide, F32),
            jax.ShapeDtypeStruct(square, F32),
            jax.ShapeDtypeStruct(rows, F32),
        ],
        compiler_params=vmem(60),
        name="feed_whole",
    )(x, att, g, bo, g2, bi, bd, win, wdown, wout)


def sum_planes_kernel(at_ref, keep_ref, got_ref, *outs):
    for r, out in enumerate(outs):
        z = at_ref[1] ^ r
        out[0] = (keep_ref[z, 0].astype(F32) + got_ref[z, 0].astype(F32)).astype(BF16)


def sum_planes(at, keep, got):
    planes, heads, rows, lanes = keep.shape
    block = pl.BlockSpec((planes, 1, rows, lanes), lambda i: (0, i, 0, 0))
    return pl.pallas_call(
        sum_planes_kernel,
        grid=(heads,),
        in_specs=[SMEM, block, block],
        out_specs=[pl.BlockSpec((1, rows, lanes), lambda i: (i, 0, 0))] * planes,
        out_shape=[jax.ShapeDtypeStruct((heads, rows, lanes), BF16)] * planes,
        compiler_params=vmem(),
        name="sum_planes",
    )(at, keep, got)


def sum_heads_kernel(at_ref, a_ref, b_ref, c_ref, d_ref, *outs):
    for r, out in enumerate(outs):
        h = at_ref[0] ^ r
        total = a_ref[h].astype(F32) + b_ref[h].astype(F32)
        out[...] = (total + c_ref[h].astype(F32) + d_ref[h].astype(F32)).astype(BF16)


def sum_heads(at, pieces):
    heads, rows, lanes = pieces[0].shape
    return pl.pallas_call(
        sum_heads_kernel,
        in_specs=[SMEM] + [VMEM] * 4,
        out_shape=[jax.ShapeDtypeStruct((rows, lanes), BF16)] * heads,
        compiler_params=vmem(),
        name="sum_heads",
    )(at, *pieces)


def last_two_kernel(a_ref, b_ref, c_ref, d_ref, gin_ref, gdown_ref, gout_ref, vec_ref):
    total = a_ref[...].astype(F32) + b_ref[...].astype(F32)
    total = total + c_ref[...].astype(F32) + d_ref[...].astype(F32)
    for k in range(2):
        gin_ref[:, k * LANES : (k + 1) * LANES] = total[k * LANES : (k + 1) * LANES]
    for k in range(4):
        gdown_ref[k * LANES : (k + 1) * LANES, :] = total[256 + k * 64 : 320 + k * 64].T
    gout_ref[...] = total[512:576].T
    vec_ref[...] = total[576:584]


def last_two(pieces):
    return pl.pallas_call(
        last_two_kernel,
        out_shape=[
            jax.ShapeDtypeStruct((LANES, 256), F32),
            jax.ShapeDtypeStruct((512, 64), F32),
            jax.ShapeDtypeStruct((LANES, 64), F32),
            jax.ShapeDtypeStruct((8, LANES), F32),
        ],
        compiler_params=vmem(),
        name="last_two",
    )(*pieces)


def last_one_kernel(a_ref, b_ref, c_ref, d_ref, gw_ref, gs_ref, vec_ref):
    total = a_ref[...].astype(F32) + b_ref[...].astype(F32)
    total = total + c_ref[...].astype(F32) + d_ref[...].astype(F32)
    gw_ref[...] = total[:192].T
    gs_ref[...] = total[192:200].T
    vec_ref[...] = total[200:208]


def last_one(pieces):
    return pl.pallas_call(
        last_one_kernel,
        out_shape=[
            jax.ShapeDtypeStruct((LANES, 192), F32),
            jax.ShapeDtypeStruct((LANES, 8), F32),
            jax.ShapeDtypeStruct((8, LANES), F32),
        ],
        compiler_params=vmem(),
        name="last_one",
    )(*pieces)


def weight_tile(gq, gkv, normed, wq_ref, wkv_ref, u_ref, gmq_ref, gmk_ref, acc_q, acc_kv, first):
    u_ref[...] = mm(gq, wq_ref[...]) + mm(gkv, wkv_ref[...])
    acc_q[...] += mm(gq.T, normed)
    acc_kv[...] += mm(gkv.T, normed)
    blocks = normed.shape[0] // BLOCK
    sums = jnp.sum(normed.astype(F32).reshape(blocks, BLOCK, D), axis=1).astype(BF16)
    rows = pl.ds(pl.multiple_of(first * blocks, blocks), blocks)
    gmq, gmk = gmq_ref[rows, :].astype(BF16), gmk_ref[rows, :].astype(BF16)
    zero = jnp.zeros((blocks, LANES), BF16)
    half = lax.broadcasted_iota(jnp.int32, (blocks, LANES), 1) < HEAD_DIM
    acc_q[...] += mm(gmq, sums, TN)
    wide = []
    for pair in range(PAIRS):
        tile = gmk[:, pair * LANES : (pair + 1) * LANES]
        wide += [jnp.where(half, tile, zero), jnp.where(half, zero, tile)]
    wide = jnp.concatenate(wide, axis=1)
    acc_kv[...] += mm(wide, sums, TN)
    block_u = mm(gmq, wq_ref[...]) + mm(wide, wkv_ref[...])
    for i in range(blocks):
        u_ref[i * BLOCK : (i + 1) * BLOCK, :] += block_u[i : i + 1]


def weight_kernel(
    fast, at_ref, gq_ref, gkv_ref, n_ref, wq_ref, wkv_ref, gmq_ref, gmk_ref, halo_ref, gain_ref,
    gs_ref, u_ref, keep_ref, send_ref, acc_q, acc_kv,
):
    @pl.when(pl.program_id(0) == 0)
    def _():
        clear(acc_q)
        acc_kv[...] = halo_ref[...]

    weight_tile(
        gq_ref[...], gkv_ref[...], n_ref[...], wq_ref, wkv_ref, u_ref, gmq_ref, gmk_ref,
        acc_q, acc_kv, pl.program_id(0),
    )

    @pl.when(pl.program_id(0) == pl.num_programs(0) - 1)
    def _():
        gain = jnp.sum(acc_q[...] * wq_ref[...].astype(F32), axis=0, keepdims=True)
        gain = gain + jnp.sum(acc_kv[...] * wkv_ref[...].astype(F32), axis=0, keepdims=True)
        gain = gain / gain_ref[...]
        if not fast:
            keep_ref[:D, :] = acc_q[...]
            keep_ref[D:, :] = acc_kv[...]
            send_ref[...] = jnp.broadcast_to(gain, (8, D))
            return
        for core in range(2):

            @pl.when(at_ref[2] == core)
            def _():
                lane = lax.broadcasted_iota(jnp.int32, (1, LANES), 1)
                for h in range(4):
                    lanes = slice(h * LANES, (h + 1) * LANES)
                    for z in range(4):
                        for c in range(2):
                            ref = keep_ref if c == core else send_ref
                            b = 2 * z + c
                            base = b * LANES
                            ref[z, h, :64, :] = acc_q[b * 64 : (b + 1) * 64, lanes].astype(BF16)
                            low = acc_kv[base : base + 64, lanes].astype(BF16)
                            high = acc_kv[base + 64 : base + 128, lanes].astype(BF16)
                            ref[z, h, 64:128, :] = low if c == 0 else high
                            ref[z, h, 128:192, :] = high if c == 0 else low
                            own = pltpu.roll(
                                jnp.broadcast_to(gain[:, lanes], (8, LANES)), -16 * b % LANES, 1
                            )
                            ref[z, h, 192:208, :] = jnp.concatenate(
                                [gs_ref[h, b * 8 : (b + 1) * 8, :], own], axis=0
                            ).astype(BF16)


def weight_back(at, gq, gkv, normed, wt_q, wt_kv, gmq, gmk, halo, gain, gsort, fast):
    tok = gq.shape[0]
    tile = 8 * BLOCK
    blocks = tok // BLOCK
    tiled = pl.BlockSpec((tile, D), lambda i: (i, 0))
    parts = (4, 4, PIECE_ONE, LANES)
    shapes = (parts, parts) if fast else ((3 * D, D), (8, D))
    kind = BF16 if fast else F32
    return pl.pallas_call(
        functools.partial(weight_kernel, fast),
        grid=(tok // tile,),
        in_specs=[
            SMEM, tiled, pl.BlockSpec((tile, 2 * D), lambda i: (i, 0)), tiled, once((D, D)),
            once((2 * D, D)), once((blocks, D)), once((blocks, D)), once((2 * D, D)),
            once((1, D)), once(gsort.shape),
        ],
        out_specs=[tiled, once(shapes[0]), once(shapes[1])],
        out_shape=[
            jax.ShapeDtypeStruct((tok, D), F32),
            jax.ShapeDtypeStruct(shapes[0], kind),
            jax.ShapeDtypeStruct(shapes[1], kind),
        ],
        scratch_shapes=[pltpu.VMEM((D, D), F32), pltpu.VMEM((2 * D, D), F32)],
        compiler_params=vmem(),
        name="weight_back",
    )(at, gq, gkv, normed, wt_q, wt_kv, gmq, gmk, halo, gain, gsort)


def finish_kernel(skip, x_ref, u_ref, one_ref, two_ref, gm_ref, gain_ref, out_ref, total):
    rows = x_ref.shape[0]
    at = lax.broadcasted_iota(jnp.int32, (rows, rows), 0)
    lane = lax.broadcasted_iota(jnp.int32, (rows, rows), 1)
    order = (lane == lax.rem(at, BLOCK) * 8 + at // BLOCK).astype(F32).astype(BF16)
    total[...] = u_ref[...] + mm(order, one_ref[...].reshape(rows, D))

    @pl.when(pl.program_id(0) >= skip)
    def _():
        total[...] += mm(order, two_ref[...].reshape(rows, D))

    x = x_ref[...].astype(F32)
    centre = x - jnp.mean(x, axis=-1, keepdims=True)
    inverse = lax.rsqrt(jnp.mean(centre * centre, axis=-1, keepdims=True) + EPSILON)
    hat = centre * inverse
    du = total[...] * gain_ref[...]
    inner = jnp.mean(du * hat, axis=-1, keepdims=True)
    out_ref[...] = gm_ref[...] + inverse * (
        du - jnp.mean(du, axis=-1, keepdims=True) - hat * inner
    )


def finish(x, u, one, two, gm, gain):
    tok = x.shape[0]
    tile = 8 * BLOCK
    skip = (tok // BLOCK - two.shape[1]) // 8
    tiled = pl.BlockSpec((tile, D), lambda i: (i, 0))
    return pl.pallas_call(
        functools.partial(finish_kernel, skip),
        grid=(tok // tile,),
        in_specs=[
            tiled, tiled,
            pl.BlockSpec((BLOCK, 8, D), lambda i: (0, i, 0)),
            pl.BlockSpec((BLOCK, 8, D), lambda i: (0, jnp.maximum(i - skip, 0), 0)),
            tiled, once((1, D)),
        ],
        out_specs=tiled,
        out_shape=jax.ShapeDtypeStruct((tok, D), F32),
        scratch_shapes=[pltpu.VMEM((tile, D), F32)],
        compiler_params=vmem(),
        name="finish",
    )(x, u, one, two, gm, gain)


class Grid:
    def __init__(self):
        self.heads = lax.axis_size("head")
        self.cycles = lax.axis_size("blk")
        self.planes = self.cycles // 2
        self.head = lax.axis_index("head")
        self.cycle = lax.axis_index("blk")
        self.plane = self.cycle // 2
        self.core = self.cycle % 2
        self.place = self.cycle * self.heads + self.head

    def send(self, value, pairs):
        return lax.ppermute(value, ("head", "blk"), pairs)

    def number(self, head, cycle):
        return head * self.cycles + cycle

    def along(self, steps):
        count = self.heads * self.cycles
        at = lambda place: self.number(place % self.heads, place // self.heads)
        return [(at(i), at(i + steps)) for i in range(count) if 0 <= i + steps < count]

    def swap_head(self, flip):
        return [
            (self.number(h, b), self.number(h ^ flip, b))
            for h in range(self.heads)
            for b in range(self.cycles)
        ]

    def swap_plane(self, flip):
        return [
            (self.number(h, b), self.number(h, b ^ (2 * flip)))
            for h in range(self.heads)
            for b in range(self.cycles)
        ]

    def swap_core(self):
        return [
            (self.number(h, b), self.number(h, b ^ 1))
            for h in range(self.heads)
            for b in range(self.cycles)
        ]


def in_order(pieces, index):
    stacked = jnp.stack(pieces)
    count = len(pieces)
    bit = 1
    while bit < count:
        swapped = jnp.stack([stacked[i ^ bit] for i in range(count)])
        stacked = jnp.where((index & bit) != 0, swapped, stacked)
        bit *= 2
    return stacked


def gather_all(grid, piece):
    got = [piece] + [grid.send(piece, grid.swap_plane(r)) for r in range(1, grid.planes)]
    got = in_order(got, grid.plane)
    got = [got] + [grid.send(got, grid.swap_head(r)) for r in range(1, grid.heads)]
    got = in_order(got, grid.head)
    got = in_order([got, grid.send(got, grid.swap_core())], grid.core)
    got = got.transpose(1, 2, 0, *range(3, got.ndim))
    return got.reshape(grid.heads, grid.cycles, *piece.shape)


def scatter_sum(grid, parts):
    mine = lax.dynamic_index_in_dim(parts, grid.core, 0, keepdims=False)
    other = lax.dynamic_index_in_dim(parts, 1 - grid.core, 0, keepdims=False)
    got = grid.send(other, grid.swap_core())
    total = (mine.astype(F32) + got.astype(F32)).astype(BF16)
    pick = lambda r: lax.dynamic_index_in_dim(total, grid.head ^ r, 0, keepdims=False)
    got = [pick(0)] + [grid.send(pick(r), grid.swap_head(r)) for r in range(1, grid.heads)]
    total = sum(item.astype(F32) for item in got).astype(BF16)
    pick = lambda r: lax.dynamic_index_in_dim(total, grid.plane ^ r, 0, keepdims=False)
    got = [pick(0)] + [grid.send(pick(r), grid.swap_plane(r)) for r in range(1, grid.planes)]
    return sum(item.astype(F32) for item in got)


def as_rows(value):
    flat = value.reshape(-1)
    short = -flat.shape[0] % LANES
    return jnp.pad(flat, (0, short)).reshape(-1, LANES)


def by_owner(grid, value):
    columns, rows = value.shape
    cut = value.reshape(grid.planes, 2, columns // grid.cycles, grid.heads, rows // grid.heads)
    return cut.transpose(1, 3, 0, 2, 4)


def vector_by_owner(grid, value):
    cut = value.reshape(grid.heads, grid.planes, 2, -1)
    return cut.transpose(2, 0, 1, 3)


def rows_of(value):
    lead = value.shape[:3]
    flat = value.reshape(*lead, -1)
    short = -flat.shape[-1] % LANES
    flat = jnp.pad(flat, ((0, 0),) * 3 + ((0, short),))
    return flat.reshape(*lead, -1, LANES)


def after(value, *others):
    return lax.optimization_barrier((value, *others))[0]


def weights_slow(grid, vectors, parameters):
    w_qkv, w_sort, w_in, w_down, w_out = parameters
    heads, cycles = grid.heads, grid.cycles
    first = jnp.concatenate([as_rows(w_qkv.T), as_rows(w_sort), as_rows(jnp.concatenate(vectors))])
    wide, sort_rows = as_rows(w_qkv.T).shape[0], as_rows(w_sort).shape[0]
    got = gather_all(grid, first)
    span = w_qkv.shape[1]
    wt_qkv = (
        got[:, :, :wide]
        .reshape(heads, cycles, span, D // heads)
        .transpose(1, 2, 0, 3)
        .reshape(HEADS, 3, HEAD_DIM, D)
    )
    wt_q = wt_qkv[:, 0].reshape(D, D)
    paired = wt_qkv.reshape(PAIRS, 2, 3, HEAD_DIM, D)
    wt_kv = jnp.stack(
        [paired[:, 0, 1], paired[:, 0, 2], paired[:, 1, 2], paired[:, 1, 1]], axis=1
    ).reshape(2 * D, D)
    size = w_sort.shape[0] * w_sort.shape[1]
    w_pairs = (
        got[:, :, wide : wide + sort_rows]
        .reshape(heads, cycles, -1)[:, :, :size]
        .reshape(heads, cycles, *w_sort.shape)
        .transpose(1, 3, 0, 2)
        .reshape(HEAD_DIM, PAIRS, LANES)
        .transpose(1, 0, 2)
        .astype(F32)
    )
    flat = got[:, :, wide + sort_rows :].reshape(heads, cycles, -1)
    sizes = [v.shape[0] for v in vectors]
    cuts = [sum(sizes[:i]) for i in range(len(sizes) + 1)]
    rows = [
        flat[:, :, cuts[i] : cuts[i + 1]].reshape(1, -1).astype(F32) for i in range(len(sizes))
    ]
    second = jnp.concatenate([as_rows(w_in.T), as_rows(w_down.T), as_rows(w_out.T)])
    in_rows, down_rows = as_rows(w_in.T).shape[0], as_rows(w_down.T).shape[0]
    got = gather_all(grid, second)

    def whole(depth, columns, part):
        return (
            part.reshape(heads, cycles, -1)[:, :, : columns // cycles * (depth // heads)]
            .reshape(heads, cycles, columns // cycles, depth // heads)
            .transpose(1, 2, 0, 3)
            .reshape(columns, depth)
        )

    feed = (
        whole(D, FF, got[:, :, :in_rows]),
        whole(FF, D, got[:, :, in_rows : in_rows + down_rows]),
        whole(D, D, got[:, :, in_rows + down_rows :]),
    )
    return wt_q, wt_kv, w_pairs, rows, feed


def matrix(rows, shape):
    flat = rows.reshape(-1)[: shape[0] * shape[1]]
    return flat.reshape(shape[1], shape[0]).T


def gradients_two_slow(grid, acc_in, acc_down, acc_out, sums, parameters, vectors):
    w_qkv, w_sort, w_in, w_down, w_out = parameters
    low = [
        rows_of(by_owner(grid, v.astype(BF16))) for v in (acc_in.T, acc_down, acc_out)
    ]
    order = ((0, D), (1, D), (4, FF), (3, D))
    small = [vector_by_owner(grid, sums[i, :n]) for i, n in order]
    low.append(rows_of(jnp.concatenate(small, axis=-1).astype(BF16)))
    total = scatter_sum(grid, jnp.concatenate(low, axis=3))
    cuts = [0]
    for item in low:
        cuts.append(cuts[-1] + item.shape[3])
    g_in, g_down, g_out = (
        matrix(total[cuts[i] : cuts[i + 1]], w.shape) for i, w in enumerate((w_in, w_down, w_out))
    )
    flat = total[cuts[3] :].reshape(-1)
    sizes = [v.shape[0] for v in vectors[1:]]
    at = [sum(sizes[:i]) for i in range(5)]
    return g_in, g_down, g_out, *(flat[at[i] : at[i + 1]] for i in range(4))


def gradients_one_slow(grid, both, gain, gsort, parameters, vectors):
    w_qkv, w_sort = parameters[:2]
    q = both[:D].reshape(HEADS, HEAD_DIM, D)
    kv = both[D:].reshape(PAIRS, 4, HEAD_DIM, D)
    k = jnp.stack([kv[:, 0], kv[:, 3]], axis=1).reshape(HEADS, HEAD_DIM, D)
    v = jnp.stack([kv[:, 1], kv[:, 2]], axis=1).reshape(HEADS, HEAD_DIM, D)
    wide = jnp.stack([q, k, v], axis=1).reshape(3 * D, D)
    sort = gsort.transpose(0, 2, 1).reshape(grid.heads, D // grid.heads, grid.planes, 2, -1)
    low = [
        rows_of(by_owner(grid, wide.astype(BF16))),
        rows_of(sort.transpose(3, 0, 2, 1, 4).astype(BF16)),
        rows_of(vector_by_owner(grid, gain[0]).astype(BF16)),
    ]
    total = scatter_sum(grid, jnp.concatenate(low, axis=3))
    one, two = low[0].shape[3], low[0].shape[3] + low[1].shape[3]
    size = w_sort.shape[0] * w_sort.shape[1]
    return (
        matrix(total[:one], w_qkv.shape),
        total[one:two].reshape(-1)[:size].reshape(w_sort.shape),
        total[two:].reshape(-1)[: vectors[0].shape[0]],
    )


def per_device(
    tokens, cotangent, doc_lengths, norm_gain1, w_qkv, w_out, b_out, norm_gain2, w_in, b_in,
    w_down, b_down, w_sort,
):
    grid = Grid()
    heads = grid.heads
    x = tokens[0]
    upstream = cotangent[0]
    tok = x.shape[0]
    own = tok // BLOCK
    context = HALO + own
    window = HALO + own + HALO
    second = HALO - own
    fast = heads == 4 and grid.cycles == 8
    at = jnp.stack([grid.head, grid.plane, grid.core]).astype(jnp.int32)
    vectors = (norm_gain1, b_out, norm_gain2, b_in, b_down)
    parameters = (w_qkv, w_sort, w_in, w_down, w_out)

    if fast:
        row = jnp.concatenate(vectors).reshape(1, LANES)
        one, two = pack(w_qkv, w_sort, row, w_in, w_down, w_out)
        ones = [one] + [grid.send(one, grid.swap_head(r)) for r in range(1, 4)]
        two = after(two, *ones)
        twos = [two] + [grid.send(two, grid.swap_head(r)) for r in range(1, 4)]
        ones = jnp.stack(ones)
        ones = [ones] + [grid.send(ones, grid.swap_plane(r)) for r in range(1, 4)]
        x_send = after(x, *twos)
    else:
        x_send = x
    halo_one = grid.send(x_send, grid.along(1))
    halo_two = grid.send(x_send[tok - second * BLOCK :], grid.along(2))
    if fast:
        ones = jnp.stack(ones)
        other = grid.send(ones, grid.swap_core())
        wt_q, wt_kv, w_pairs, *rows = assemble(at, ones, other)
        twos = after(jnp.stack(twos), other)
        twos = jnp.stack([twos] + [grid.send(twos, grid.swap_plane(r)) for r in range(1, 4)])
        feed_weights = (twos, grid.send(twos, grid.swap_core()))
    else:
        wt_q, wt_kv, w_pairs, rows, feed_weights = weights_slow(grid, vectors, parameters)
    gain_one, bias_out, gain_two, bias_in, bias_down = rows

    normed, q, kv, q_mean, k_mean = project(x, gain_one, wt_q, wt_kv)
    means = jnp.concatenate([q_mean, k_mean], axis=1)
    means_window = jnp.concatenate(
        [
            grid.send(means[own - second :], grid.along(2)),
            grid.send(means, grid.along(1)),
            means,
            grid.send(means, grid.along(-1)),
            grid.send(means[:second], grid.along(-2)),
        ]
    )
    x_context = jnp.concatenate([halo_two, halo_one, x]).reshape(context, BLOCK, D)

    begin = grid.place * own
    position = begin - HALO + jnp.arange(window, dtype=jnp.int32)
    doc_ends = jnp.cumsum(doc_lengths, dtype=jnp.int32)
    ended = jnp.sum(
        (doc_ends[None, :] <= position[:, None]).astype(jnp.int32), axis=1, dtype=jnp.int32
    )
    span_end = (grid.cycle + 1) * heads * own
    doc = jnp.where((position >= 0) & (position < span_end), ended, -1)
    fold = window - LANES
    docc = jnp.stack([doc[:LANES], jnp.concatenate([doc[LANES:], doc[fold:LANES]])])
    docn = doc[:, None]
    live = (doc[HALO:context] == doc[HALO - 1 : context - 1]) & (doc[HALO:context] >= 0)
    live = jnp.repeat(live.astype(F32), BLOCK).reshape(tok // LANES, LANES)

    q_window, k_window = means_window[:, :D], means_window[:, D:]
    plan = sink_forward(q_window, k_window, w_pairs, docn, docc, own, context)
    kvx, normed_halo = context_project(x_context, gain_one, wt_kv, HALO)
    attended, skv = attend(q, kv, kvx, plan, live)

    if fast:
        output, g_middle, g_att, keep, send = feed_fast(
            at, x, attended, upstream, bias_out, gain_two, bias_in, bias_down, *feed_weights
        )
        got = grid.send(send, grid.swap_core())
        twos = sum_planes(at, keep, got)
        twos = [twos[0]] + [grid.send(twos[r], grid.swap_plane(r)) for r in range(1, 4)]
    else:
        output, g_middle, g_att, *sums = feed_slow(
            x, attended, upstream, bias_out, gain_two, bias_in, bias_down, *feed_weights
        )
        g_in, g_down, g_out, g_b_out, g_gain_two, g_b_in, g_b_down = gradients_two_slow(
            grid, *sums, parameters, vectors
        )

    gq, gkv, gh, gplan = attend_back(q, kv, skv, g_att, kvx, plan, live)
    gn_halo, g_kv_halo = halo_back(gh, normed_halo, wt_kv)
    back_one = grid.send(gn_halo[:, second:], grid.along(-1))
    back_two = grid.send(gn_halo[:, :second], grid.along(-2))
    gq_window, gk_window, gsort = sink_backward(
        q_window, k_window, w_pairs, docn, docc, gplan, own, context
    )
    gmeans = jnp.concatenate([gq_window, gk_window], axis=1) / BLOCK
    gmeans_low = gmeans.astype(BF16)
    total = (
        gmeans[HALO:context]
        + grid.send(gmeans_low[second:HALO], grid.along(-1)).astype(F32)
        + grid.send(gmeans_low[context : context + own], grid.along(1)).astype(F32)
    )
    far_left = grid.send(gmeans_low[:second], grid.along(-2)).astype(F32)
    far_right = grid.send(gmeans_low[context + own :], grid.along(2)).astype(F32)
    total = total + jnp.pad(far_left, ((own - second, 0), (0, 0)))
    total = total + jnp.pad(far_right, ((0, own - second), (0, 0)))
    u, keep, send = weight_back(
        at, gq, gkv, normed, wt_q, wt_kv, total[:, :D], total[:, D:], g_kv_halo, gain_one, gsort,
        fast,
    )
    if fast:
        got = grid.send(send, grid.swap_core())
        ones = sum_planes(at, keep, got)
        ones = [ones[0]] + [grid.send(ones[r], grid.swap_plane(r)) for r in range(1, 4)]
        ones = sum_heads(at, ones)
        ones = [ones[0]] + [grid.send(ones[r], grid.swap_head(r)) for r in range(1, 4)]
        g_wqkv, g_sort, vec_one = last_one(ones)
        g_gain_one = vec_one[0, :16]
        twos = sum_heads(at, twos)
        twos = [twos[0]] + [grid.send(twos[r], grid.swap_head(r)) for r in range(1, 4)]
        g_in, g_down, g_out, vec_two = last_two(twos)
        g_b_out, g_gain_two = vec_two[0, 16:32], vec_two[0, 32:48]
        g_b_in, g_b_down = vec_two[0, 48:112], vec_two[0, 112:]
    else:
        g_wqkv, g_sort, g_gain_one = gradients_one_slow(
            grid, keep, send, gsort, parameters, vectors
        )
    input_grad = finish(x, u, back_one, back_two, g_middle, gain_one)
    return (
        output[None], input_grad[None], g_gain_one, g_wqkv, g_out, g_b_out, g_gain_two, g_in,
        g_b_in, g_down, g_b_down, g_sort,
    )


def solution(mesh):
    both = P(("head", "blk"))
    split = P("head", "blk")
    stream = P("blk", "head", None)
    return jax.shard_map(
        per_device,
        mesh=mesh,
        in_specs=(
            stream, stream, P(), both, split, split, both, both, split, both, split, both, split,
        ),
        out_specs=(
            stream, stream, both, split, split, both, both, split, both, split, both, split,
        ),
        check_vma=False,
    )
```

time: 887 us -> 509 us (0.57)
  Pallas kernels: 0 us -> 219 us
  blocking collectives: 179 us -> 0 us
  local copies, waits for them, and re-layouts: 200 us -> 33.5 us
  other arithmetic: 153 us -> 9.8 us
  matrix products: 143 us -> 0 us
  starting transfers between devices: 34.4 us -> 112 us
  between operations: 29.5 us -> 1.62 us
  waiting for transfers between devices: 138 us -> 124 us
    pallas_call x0 -> x18, Pallas kernels: none -> 219 us  [the longest x1 41.6 us: attend_back(): pl.pallas_call(attend_back_kernel, grid=(PAIRS,), in_specs=[pl.BlockSpec(...]
    dot_general x33 -> x0, matrix products: 143 us -> none  [the longest x1 14 us: per_device(): jnp.einsum('td,fd->tf', upstream, weight_down, preferred_element_type=jnp...]
    all_gather x11 -> x0, blocking collectives: 123 us -> none  [the longest x1 16 us: per_device(): lax.all_gather(w_qkv, 'blk', axis=1, tiled=True)]
    ppermute x4 -> x40, waiting for transfers between devices: 2.04 us -> 124 us  [send(): return lax.ppermute(value, ('head', 'blk'), pairs)]
    ppermute x4 -> x40, starting transfers between devices: 12.3 us -> 112 us  [send(): return lax.ppermute(value, ('head', 'blk'), pairs)]
    sub x1 -> x0, other arithmetic: 69.7 us -> none  [per_device(): grad_weights - jnp.sum(weights * grad_weights, axis=-1, keepdims=True)]
    unnamed x14 -> x0, waiting for transfers between devices: 64 us -> none
    unnamed x3 -> x0, blocking collectives: 55.5 us -> none
  transfers between devices with their start and end apart: 19 -> 40, of which waited for: 8 -> 21; matrix products, arithmetic and copies ran while one was open for 48% -> 4% of each run, Pallas kernels for 0% -> 35%
where the time goes in v1:
time: 509 us; the launch traced here: 499 us
  Pallas kernels  219 us (43%)
  waiting for transfers between devices  124 us (24%)
  starting transfers between devices  112 us (22%)
  local copies, waits for them, and re-layouts  33.5 us (7%)
  other arithmetic  9.8 us (2%)
    ppermute x40, waiting for transfers between devices, send(): return lax.ppermute(value, ('head', 'blk'), pairs)  124 us
    ppermute x40, starting transfers between devices, send(): return lax.ppermute(value, ('head', 'blk'), pairs)  112 us
    pallas_call x1, Pallas kernels, attend_back(): pl.pallas_call(attend_back_kernel, grid=(PAIRS,), in_specs=[pl.BlockSpec(...  41.6 us
    pallas_call x1, Pallas kernels, feed_fast(): pl.pallas_call(feed_fast_kernel, grid=(tok // tile,), in_specs=[SMEM, til...  38.1 us
    pallas_call x1, Pallas kernels, attend(): pl.pallas_call(attend_kernel, grid=(PAIRS,), in_specs=[pl.BlockSpec((tok,...  27.9 us
    pallas_call x1, Pallas kernels, sink_backward(): pl.pallas_call(functools.partial(sink_backward_kernel, own, context), out...  20 us
    unnamed x50, local copies, waits for them, and re-layouts  19.1 us
    pallas_call x1, Pallas kernels, context_project(): pl.pallas_call(functools.partial(context_kernel, halo_blocks), grid=(BLOC...  17.3 us
  transfers between devices with their start and end apart: 40, of which 21 were waited for; matrix products, arithmetic and copies ran while one was open for 4% of the time, Pallas kernels for 35%

profile of v1, /device:TPU:12, one launch (start us, length us, event | category | flops | bytes accessed | tf_op | source)
XLA Modules:
  0.0 498.7 jit_solution(18394022956651891794)
XLA Ops:
  6.6 3.9 concatenate.18
  24.1 4.6 collective-permute-done.3
  28.6 8.6 %collective-permute-done.4 = bf16[4,208,128]{2,1,0:T(8,128)(2,1)S(1)} collective-permute-done((bf16[4,208,128]{2,1,0:T(8,128)(2,1)S(1)}, bf16[4,208,128]{2,1,0:T(8,128)(2,1)S(1)}, u32[]{:S(2)}, u32[]{:S(2)}) %collective-permute-start.4) | collective-permute-done | bytes 213024 | tf_op jit(solution)/shard_map/ppermute | solution.py:1136
  58.1 18.5 %collective-permute-done.16 = bf16[4,576,128]{2,1,0:T(8,128)(2,1)S(1)} collective-permute-done((bf16[4,576,128]{2,1,0:T(8,128)(2,1)S(1)}, bf16[4,576,128]{2,1,0:T(8,128)(2,1)S(1)}, u32[]{:S(2)}, u32[]{:S(2)}) %collective-permute-start.16) | collective-permute-done | bytes 589856 | tf_op jit(solution)/shard_map/ppermute | solution.py:1136
  76.6 17.6 %collective-permute-done.17 = bf16[4,576,128]{2,1,0:T(8,128)(2,1)S(1)} collective-permute-done((bf16[4,576,128]{2,1,0:T(8,128)(2,1)S(1)}, bf16[4,576,128]{2,1,0:T(8,128)(2,1)S(1)}, u32[]{:S(2)}, u32[]{:S(2)}) %collective-permute-start.17) | collective-permute-done | bytes 589856 | tf_op jit(solution)/shard_map/ppermute | solution.py:1136
  94.2 12.1 %collective-permute-done.18 = bf16[4,576,128]{2,1,0:T(8,128)(2,1)} collective-permute-done((bf16[4,576,128]{2,1,0:T(8,128)(2,1)S(1)}, bf16[4,576,128]{2,1,0:T(8,128)(2,1)}, u32[]{:S(2)}, u32[]{:S(2)}) %collective-permute-start.18) | collective-permute-done | bytes 589856 | tf_op jit(solution)/shard_map/ppermute | solution.py:1136
  114.1 7.8 %project.1 = (bf16[1536,512]{1,0:T(8,128)(2,1)}, bf16[1536,512]{1,0:T(8,128)(2,1)}, bf16[1536,1024]{1,0:T(8,128)(2,1)}, f32[48,512]{1,0:T(8,128)}, f32[48,512]{1,0:T(8,128)}) custom-call(bf16[1536,512]{1,0:T(8,128)(2,1)} %bitcast.3.x_ref, f32[1,512]{1,0:T(1,128)} %get-tuple-element.75.gain_ref, bf16[512,512]{1,0:T(8,128)(2,1)} %get-tuple-element.76.wq_ref, ...), custom_call_target="tpu_custom_call" | custom-call | tf_op jit(solution)/shard_map/project/pallas_call | solution.py:576
  134.6 22.9 %collective-permute-done.12 = f32[16,1024]{1,0:T(8,128)S(1)} collective-permute-done((f32[16,1024]{1,0:T(8,128)S(1)}, f32[16,1024]{1,0:T(8,128)S(1)}, u32[]{:S(2)}, u32[]{:S(2)}) %collective-permute-start.12) | collective-permute-done | bytes 65568 | tf_op jit(solution)/shard_map/ppermute | solution.py:1136
  166.8 12.5 %sink_forward.1.plan_ref = bf16[8,48,128]{2,1,0:T(8,128)(2,1)} custom-call(f32[176,512]{1,0:T(8,128)} %get-tuple-element.175.q_ref, f32[176,512]{1,0:T(8,128)} %get-tuple-element.174.k_ref, f32[4,64,128]{2,1,0:T(8,128)} %get-tuple-element.86.w_ref, s32[176,1]{1,0:T(8,128)} %fusion.6.docn_ref, s32[2,128]{1,0:T(2,128)} %pad_add_fusion.docc_ref), custom_call_target="tpu_custom_call" | custom-call | tf_op jit(solution)/shard_map/sink_forward/pallas_call | solution.py:208
  182.4 17.3 %context_project.1 = (bf16[8,112,4096]{2,1,0:T(8,128)(2,1)}, bf16[32,64,512]{2,1,0:T(8,128)(2,1)}) custom-call(bf16[112,32,512]{2,1,0:T(8,128)(2,1)} %bitcast.42, f32[1,512]{1,0:T(1,128)} %get-tuple-element.75.gain_ref, bf16[1024,512]{1,0:T(8,128)(2,1)} %get-tuple-element.77.wkv_ref.w_ref), custom_call_target="tpu_custom_call" | custom-call | tf_op jit(solution)/shard_map/context_project/pallas_call | solution.py:264
  199.7 27.9 %attend.1 = (bf16[1536,512]{1,0:T(8,128)(2,1)}, bf16[1536,1024]{1,0:T(8,128)(2,1)}) custom-call(bf16[1536,512]{1,0:T(8,128)(2,1)} %get-tuple-element.78.q_ref, bf16[1536,1024]{1,0:T(8,128)(2,1)} %get-tuple-element.79.kv_ref, bf16[8,112,4096]{2,1,0:T(8,128)(2,1)} %get-tuple-element.83.kvx_ref, bf16[8,48,128]{2,1,0:T(8,128)(2,1)} %sink_forward.1.plan_ref, ...), custom_call_target="tpu_custom_call" | custom-call | tf_op jit(solution)/shard_map/attend/pallas_call | solution.py:361
  229.1 38.1 %feed.1 = (bf16[1536,512]{1,0:T(8,128)(2,1)}, f32[1536,512]{1,0:T(8,128)}, bf16[1536,512]{1,0:T(8,128)(2,1)}, bf16[4,4,592,128]{3,2,1,0:T(8,128)(2,1)}, bf16[4,4,592,128]{3,2,1,0:T(8,128)(2,1)}) custom-call(s32[3]{0:T(128)} %pad_add_fusion.1.at_ref, bf16[1536,512]{1,0:T(8,128)(2,1)} %bitcast.3.x_ref, bf16[1536,512]{1,0:T(8,128)(2,1)} %get-tuple-element.87.att_ref, ...), custom_call_target="tpu_custom_call" | custom-call | tf_op jit(solution)/shard_map/feed/pallas_call | solution.py:831
  267.3 41.6 %attend_back.1 = (bf16[1536,512]{1,0:T(8,128)(2,1)}, bf16[1536,1024]{1,0:T(8,128)(2,1)}, bf16[8,64,4096]{2,1,0:T(8,128)(2,1)}, f32[8,48,128]{2,1,0:T(8,128)}) custom-call(bf16[1536,512]{1,0:T(8,128)(2,1)} %get-tuple-element.78.q_ref, bf16[1536,1024]{1,0:T(8,128)(2,1)} %get-tuple-element.79.kv_ref, bf16[1536,1024]{1,0:T(8,128)(2,1)} %get-tuple-element.94.skv_ref, ...), custom_call_target="tpu_custom_call" | custom-call | tf_op jit(solution)/shard_map/attend_back/pallas_call | solution.py:480
  308.9 20.0 %sink_backward.1 = (f32[176,512]{1,0:T(8,128)}, f32[176,512]{1,0:T(8,128)}, f32[4,64,128]{2,1,0:T(8,128)}) custom-call(f32[176,512]{1,0:T(8,128)} %get-tuple-element.175.q_ref, f32[176,512]{1,0:T(8,128)} %get-tuple-element.174.k_ref, f32[4,64,128]{2,1,0:T(8,128)} %get-tuple-element.86.w_ref, s32[176,1]{1,0:T(8,128)} %fusion.6.docn_ref, ...), custom_call_target="tpu_custom_call" | custom-call | tf_op jit(solution)/shard_map/sink_backward/pallas_call | solution.py:219
  330.1 4.2 collective-permute-start.20
  341.9 8.6 %halo_back.1 = (bf16[32,64,512]{2,1,0:T(8,128)(2,1)}, f32[1024,512]{1,0:T(8,128)}) custom-call(bf16[8,64,4096]{2,1,0:T(8,128)(2,1)} %get-tuple-element.102.gh_ref, bf16[32,64,512]{2,1,0:T(8,128)(2,1)} %get-tuple-element.103.nh_ref, bf16[1024,512]{1,0:T(8,128)(2,1)} %get-tuple-element.77.wkv_ref.w_ref), custom_call_target="tpu_custom_call" | custom-call | tf_op jit(solution)/shard_map/halo_back/pallas_call | solution.py:532
  351.3 15.1 %weight_back.1 = (f32[1536,512]{1,0:T(8,128)}, bf16[4,4,208,128]{3,2,1,0:T(8,128)(2,1)}, bf16[4,4,208,128]{3,2,1,0:T(8,128)(2,1)}) custom-call(s32[3]{0:T(128)} %pad_add_fusion.1.at_ref, bf16[1536,512]{1,0:T(8,128)(2,1)} %get-tuple-element.96.gq_ref, bf16[1536,1024]{1,0:T(8,128)(2,1)} %get-tuple-element.97.gkv_ref, ...), custom_call_target="tpu_custom_call" | custom-call | tf_op jit(solution)/shard_map/weight_back/pallas_call | solution.py:1060
  367.3 4.5 collective-permute-start.24
  380.3 4.4 sum_planes.3
  388.0 5.6 %collective-permute-done.28.c_ref = bf16[4,208,128]{2,1,0:T(8,128)(2,1)S(1)} collective-permute-done((bf16[4,208,128]{2,1,0:T(8,128)(2,1)}, bf16[4,208,128]{2,1,0:T(8,128)(2,1)S(1)}, u32[]{:S(2)}, u32[]{:S(2)}) %collective-permute-start.28) | collective-permute-done | bytes 213024 | tf_op jit(solution)/shard_map/ppermute | solution.py:1136
  393.9 5.2 %collective-permute-done.29.d_ref = bf16[4,208,128]{2,1,0:T(8,128)(2,1)} collective-permute-done((bf16[4,208,128]{2,1,0:T(8,128)(2,1)}, bf16[4,208,128]{2,1,0:T(8,128)(2,1)}, u32[]{:S(2)}, u32[]{:S(2)}) %collective-permute-start.29) | collective-permute-done | bytes 213024 | tf_op jit(solution)/shard_map/ppermute | solution.py:1136
  402.1 6.1 %collective-permute-done.30.b_ref = bf16[208,128]{1,0:T(8,128)(2,1)S(1)} collective-permute-done((bf16[208,128]{1,0:T(8,128)(2,1)}, bf16[208,128]{1,0:T(8,128)(2,1)S(1)}, u32[]{:S(2)}, u32[]{:S(2)}) %collective-permute-start.30) | collective-permute-done | bytes 53280 | tf_op jit(solution)/shard_map/ppermute | solution.py:1136
  408.2 47.6 %collective-permute-start.31 = (bf16[208,128]{1,0:T(8,128)(2,1)}, bf16[208,128]{1,0:T(8,128)(2,1)S(1)}, u32[]{:S(2)}, u32[]{:S(2)}) collective-permute-start(bf16[208,128]{1,0:T(8,128)(2,1)} %get-tuple-element.117), channel_id=1, source_target_pairs={{0,16},{1,17},{2,18},{3,19},{4,20},{5,21},{6,22},{7,23},{8,24},{9,... | collective-permute-start | bytes 159752 | tf_op jit(solution)/shard_map/ppermute | solution.py:1136
  481.2 8.4 %finish.1 = f32[1536,512]{1,0:T(8,128)} custom-call(bf16[1536,512]{1,0:T(8,128)(2,1)} %bitcast.3.x_ref, f32[1536,512]{1,0:T(8,128)} %get-tuple-element.106.u_ref, bf16[32,48,512]{2,1,0:T(8,128)(2,1)} %copy-done.5, bf16[32,16,512]{2,1,0:T(8,128)(2,1)} %collective-permute-done.25.two_ref, f32[1536,512]{1,0:T(8,128)} %get-tuple-element.108.gm_ref, ...), custom_call_target="tpu_custom_call" | custom-call | tf_op jit(solution)/shard_map/finish/pallas_call | solution.py:1107
  (163 shorter events, 133.9 us)
Async XLA Ops:
  21.0 16.2 %collective-permute-start.4 = (bf16[4,208,128]{2,1,0:T(8,128)(2,1)S(1)}, bf16[4,208,128]{2,1,0:T(8,128)(2,1)S(1)}, u32[]{:S(2)}, u32[]{:S(2)}) collective-permute-start(bf16[4,208,128]{2,1,0:T(8,128)(2,1)S(1)} %get-tuple-element.181), channel_id=1, source_target_pairs={{0,4},{1,5},{2,6},{3,7},{4,0},{5,1},{6,2},{7,3},{8,12},{9,13},{10,... | collective-permute-start | bytes 638984 | tf_op jit(solution)/shard_map/ppermute | solution.py:1136
  23.6 17.2 %collective-permute-start.5 = (bf16[4,208,128]{2,1,0:T(8,128)(2,1)S(1)}, bf16[4,208,128]{2,1,0:T(8,128)(2,1)S(1)}, u32[]{:S(2)}, u32[]{:S(2)}) collective-permute-start(bf16[4,208,128]{2,1,0:T(8,128)(2,1)S(1)} %get-tuple-element.181), channel_id=1, source_target_pairs={{0,6},{1,7},{2,4},{3,5},{4,2},{5,3},{6,0},{7,1},{8,14},{9,15},{10,... | collective-permute-start | bytes 638984 | tf_op jit(solution)/shard_map/ppermute | solution.py:1136
  52.0 24.6 %collective-permute-start.16 = (bf16[4,576,128]{2,1,0:T(8,128)(2,1)S(1)}, bf16[4,576,128]{2,1,0:T(8,128)(2,1)S(1)}, u32[]{:S(2)}, u32[]{:S(2)}) collective-permute-start(bf16[4,576,128]{2,1,0:T(8,128)(2,1)S(1)} %pad_maximum_fusion.3), channel_id=1, source_target_pairs={{0,2},{1,3},{2,0},{3,1},{4,6},{5,7},{6,4},{7,5},{8,10},{9,11},{10,... | collective-permute-start | bytes 1769480 | tf_op jit(solution)/shard_map/ppermute | solution.py:1136
  52.1 42.1 %collective-permute-start.17 = (bf16[4,576,128]{2,1,0:T(8,128)(2,1)S(1)}, bf16[4,576,128]{2,1,0:T(8,128)(2,1)S(1)}, u32[]{:S(2)}, u32[]{:S(2)}) collective-permute-start(bf16[4,576,128]{2,1,0:T(8,128)(2,1)S(1)} %pad_maximum_fusion.3), channel_id=1, source_target_pairs={{0,4},{1,5},{2,6},{3,7},{4,0},{5,1},{6,2},{7,3},{8,12},{9,13},{10,... | collective-permute-start | bytes 1769480 | tf_op jit(solution)/shard_map/ppermute | solution.py:1136
  55.1 51.1 %collective-permute-start.18 = (bf16[4,576,128]{2,1,0:T(8,128)(2,1)S(1)}, bf16[4,576,128]{2,1,0:T(8,128)(2,1)}, u32[]{:S(2)}, u32[]{:S(2)}) collective-permute-start(bf16[4,576,128]{2,1,0:T(8,128)(2,1)S(1)} %pad_maximum_fusion.3), channel_id=1, source_target_pairs={{0,6},{1,7},{2,4},{3,5},{4,2},{5,3},{6,0},{7,1},{8,14},{9,15},{10,... | collective-permute-start | bytes 1769480 | tf_op jit(solution)/shard_map/ppermute | solution.py:1136
  107.7 119.9 %collective-permute-start.19 = (bf16[4,4,576,128]{3,2,1,0:T(8,128)(2,1)S(1)}, bf16[4,4,576,128]{3,2,1,0:T(8,128)(2,1)S(1)}, u32[]{:S(2)}, u32[]{:S(2)}) collective-permute-start(bf16[4,4,576,128]{3,2,1,0:T(8,128)(2,1)S(1)} %pad_maximum_fusion.1.mine_ref), channel_id=1, source_target_pairs={{0,1},{1,0},{2,3},{3,2},{4,5},{5,4},{6,7},{7,6},{8,9},{9,8},{10,11... | collective-permute-start | bytes 7077896 | tf_op jit(solution)/shard_map/ppermute | solution.py:1136
  107.8 71.5 %collective-permute-start.11 = (bf16[1536,512]{1,0:T(8,128)(2,1)}, bf16[1536,512]{1,0:T(8,128)(2,1)S(1)}, u32[]{:S(2)}, u32[]{:S(2)}) collective-permute-start(bf16[1536,512]{1,0:T(8,128)(2,1)} %bitcast.3.x_ref), channel_id=1, source_target_pairs={{0,8},{8,16},{16,24},{24,1},{1,9},{9,17},{17,25},{25,2},{2,10},{10... | collective-permute-start | bytes 4718600 | tf_op jit(solution)/shard_map/ppermute | solution.py:1136
  123.8 35.7 %collective-permute-start.13 = (f32[48,1024]{1,0:T(8,128)S(1)}, f32[48,1024]{1,0:T(8,128)S(1)}, u32[]{:S(2)}, u32[]{:S(2)}) collective-permute-start(f32[48,1024]{1,0:T(8,128)S(1)} %constant_dynamic-update-slice_fusion), channel_id=1, source_target_pairs={{0,8},{8,16},{16,24},{24,1},{1,9},{9,17},{17,25},{25,2},{2,10},{10... | collective-permute-start | bytes 589832 | tf_op jit(solution)/shard_map/ppermute | solution.py:1136
  127.0 30.5 %collective-permute-start.12 = (f32[16,1024]{1,0:T(8,128)S(1)}, f32[16,1024]{1,0:T(8,128)S(1)}, u32[]{:S(2)}, u32[]{:S(2)}) collective-permute-start(f32[16,1024]{1,0:T(8,128)S(1)} %get-tuple-element.185), channel_id=1, source_target_pairs={{0,16},{8,24},{16,1},{24,9},{1,17},{9,25},{17,2},{25,10},{2,18},{1... | collective-permute-start | bytes 196616 | tf_op jit(solution)/shard_map/ppermute | solution.py:1136
  131.5 47.8 %collective-permute-start.10 = (bf16[512,512]{1,0:T(8,128)(2,1)S(1)}, bf16[512,512]{1,0:T(8,128)(2,1)S(1)}, u32[]{:S(2)}, u32[]{:S(2)}) collective-permute-start(bf16[512,512]{1,0:T(8,128)(2,1)S(1)} %slice.78), channel_id=1, source_target_pairs={{0,16},{8,24},{16,1},{24,9},{1,17},{9,25},{17,2},{25,10},{2,18},{1... | collective-permute-start | bytes 1572872 | tf_op jit(solution)/shard_map/ppermute | solution.py:1136
  267.2 111.7 %collective-permute-start.33 = (bf16[4,4,592,128]{3,2,1,0:T(8,128)(2,1)}, bf16[4,4,592,128]{3,2,1,0:T(8,128)(2,1)S(1)}, u32[]{:S(2)}, u32[]{:S(2)}) collective-permute-start(bf16[4,4,592,128]{3,2,1,0:T(8,128)(2,1)} %get-tuple-element.122), channel_id=1, source_target_pairs={{0,1},{1,0},{2,3},{3,2},{4,5},{5,4},{6,7},{7,6},{8,9},{9,8},{10,11... | collective-permute-start | bytes 7274504 | tf_op jit(solution)/shard_map/ppermute | solution.py:1136
  330.1 20.4 %collective-permute-start.20 = (bf16[48,1024]{1,0:T(8,128)(2,1)S(1)}, bf16[48,1024]{1,0:T(8,128)(2,1)S(1)}, u32[]{:S(2)}, u32[]{:S(2)}) collective-permute-start(bf16[48,1024]{1,0:T(8,128)(2,1)S(1)} %get-tuple-element.178), channel_id=1, source_target_pairs={{8,0},{16,8},{24,16},{1,24},{9,1},{17,9},{25,17},{2,25},{10,2},{18... | collective-permute-start | bytes 294920 | tf_op jit(solution)/shard_map/ppermute | solution.py:1136
  334.4 16.2 %collective-permute-start.21 = (bf16[48,1024]{1,0:T(8,128)(2,1)S(1)}, bf16[48,1024]{1,0:T(8,128)(2,1)S(1)}, u32[]{:S(2)}, u32[]{:S(2)}) collective-permute-start(bf16[48,1024]{1,0:T(8,128)(2,1)S(1)} %get-tuple-element.179), channel_id=1, source_target_pairs={{0,8},{8,16},{16,24},{24,1},{1,9},{9,17},{17,25},{25,2},{2,10},{10... | collective-permute-start | bytes 294920 | tf_op jit(solution)/shard_map/ppermute | solution.py:1136
  367.3 112.8 %collective-permute-start.24 = (bf16[32,48,512]{2,1,0:T(8,128)(2,1)S(1)}, bf16[32,48,512]{2,1,0:T(8,128)(2,1)S(1)}, u32[]{:S(2)}, u32[]{:S(2)}) collective-permute-start(bf16[32,48,512]{2,1,0:T(8,128)(2,1)S(1)} %slice.96), channel_id=1, source_target_pairs={{8,0},{16,8},{24,16},{1,24},{9,1},{17,9},{25,17},{2,25},{10,2},{18... | collective-permute-start | bytes 4718600 | tf_op jit(solution)/shard_map/ppermute | solution.py:1136
  375.4 18.2 %collective-permute-start.28 = (bf16[4,208,128]{2,1,0:T(8,128)(2,1)}, bf16[4,208,128]{2,1,0:T(8,128)(2,1)S(1)}, u32[]{:S(2)}, u32[]{:S(2)}) collective-permute-start(bf16[4,208,128]{2,1,0:T(8,128)(2,1)} %get-tuple-element.113), channel_id=1, source_target_pairs={{0,4},{1,5},{2,6},{3,7},{4,0},{5,1},{6,2},{7,3},{8,12},{9,13},{10,... | collective-permute-start | bytes 638984 | tf_op jit(solution)/shard_map/ppermute | solution.py:1136
  378.4 20.6 %collective-permute-start.29 = (bf16[4,208,128]{2,1,0:T(8,128)(2,1)}, bf16[4,208,128]{2,1,0:T(8,128)(2,1)}, u32[]{:S(2)}, u32[]{:S(2)}) collective-permute-start(bf16[4,208,128]{2,1,0:T(8,128)(2,1)} %get-tuple-element.114), channel_id=1, source_target_pairs={{0,6},{1,7},{2,4},{3,5},{4,2},{5,3},{6,0},{7,1},{8,14},{9,15},{10,... | collective-permute-start | bytes 638984 | tf_op jit(solution)/shard_map/ppermute | solution.py:1136
  384.7 87.5 %collective-permute-start.34 = (bf16[4,592,128]{2,1,0:T(8,128)(2,1)}, bf16[4,592,128]{2,1,0:T(8,128)(2,1)}, u32[]{:S(2)}, u32[]{:S(2)}) collective-permute-start(bf16[4,592,128]{2,1,0:T(8,128)(2,1)} %get-tuple-element.124), channel_id=1, source_target_pairs={{0,2},{1,3},{2,0},{3,1},{4,6},{5,7},{6,4},{7,5},{8,10},{9,11},{10,... | collective-permute-start | bytes 1818632 | tf_op jit(solution)/shard_map/ppermute | solution.py:1136
  385.7 86.5 %collective-permute-start.35 = (bf16[4,592,128]{2,1,0:T(8,128)(2,1)}, bf16[4,592,128]{2,1,0:T(8,128)(2,1)}, u32[]{:S(2)}, u32[]{:S(2)}) collective-permute-start(bf16[4,592,128]{2,1,0:T(8,128)(2,1)} %get-tuple-element.125), channel_id=1, source_target_pairs={{0,4},{1,5},{2,6},{3,7},{4,0},{5,1},{6,2},{7,3},{8,12},{9,13},{10,... | collective-permute-start | bytes 1818632 | tf_op jit(solution)/shard_map/ppermute | solution.py:1136
  393.6 78.6 %collective-permute-start.36 = (bf16[4,592,128]{2,1,0:T(8,128)(2,1)}, bf16[4,592,128]{2,1,0:T(8,128)(2,1)}, u32[]{:S(2)}, u32[]{:S(2)}) collective-permute-start(bf16[4,592,128]{2,1,0:T(8,128)(2,1)} %get-tuple-element.126), channel_id=1, source_target_pairs={{0,6},{1,7},{2,4},{3,5},{4,2},{5,3},{6,0},{7,1},{8,14},{9,15},{10,... | collective-permute-start | bytes 1818632 | tf_op jit(solution)/shard_map/ppermute | solution.py:1136
  408.2 50.0 %collective-permute-start.31 = (bf16[208,128]{1,0:T(8,128)(2,1)}, bf16[208,128]{1,0:T(8,128)(2,1)S(1)}, u32[]{:S(2)}, u32[]{:S(2)}) collective-permute-start(bf16[208,128]{1,0:T(8,128)(2,1)} %get-tuple-element.117), channel_id=1, source_target_pairs={{0,16},{1,17},{2,18},{3,19},{4,20},{5,21},{6,22},{7,23},{8,24},{9,... | collective-permute-start | bytes 159752 | tf_op jit(solution)/shard_map/ppermute | solution.py:1136
  463.4 16.6 %collective-permute-start.25 = (bf16[32,16,512]{2,1,0:T(8,128)(2,1)}, bf16[32,16,512]{2,1,0:T(8,128)(2,1)}, u32[]{:S(2)}, u32[]{:S(2)}) collective-permute-start(bf16[32,16,512]{2,1,0:T(8,128)(2,1)} %slice.97), channel_id=1, source_target_pairs={{16,0},{24,8},{1,16},{9,24},{17,1},{25,9},{2,17},{10,25},{18,2},{2... | collective-permute-start | bytes 1572872 | tf_op jit(solution)/shard_map/ppermute | solution.py:1136
  474.9 14.7 %collective-permute-start.37 = (bf16[592,128]{1,0:T(8,128)(2,1)}, bf16[592,128]{1,0:T(8,128)(2,1)S(1)}, u32[]{:S(2)}, u32[]{:S(2)}) collective-permute-start(bf16[592,128]{1,0:T(8,128)(2,1)} %get-tuple-element.128), channel_id=1, source_target_pairs={{0,8},{1,9},{2,10},{3,11},{4,12},{5,13},{6,14},{7,15},{8,0},{9,1},... | collective-permute-start | bytes 454664 | tf_op jit(solution)/shard_map/ppermute | solution.py:1136
  474.9 14.7 %collective-permute-start.38 = (bf16[592,128]{1,0:T(8,128)(2,1)}, bf16[592,128]{1,0:T(8,128)(2,1)S(1)}, u32[]{:S(2)}, u32[]{:S(2)}) collective-permute-start(bf16[592,128]{1,0:T(8,128)(2,1)} %get-tuple-element.129), channel_id=1, source_target_pairs={{0,16},{1,17},{2,18},{3,19},{4,20},{5,21},{6,22},{7,23},{8,24},{9,... | collective-permute-start | bytes 454664 | tf_op jit(solution)/shard_map/ppermute | solution.py:1136
  475.0 14.6 %collective-permute-start.39 = (bf16[592,128]{1,0:T(8,128)(2,1)}, bf16[592,128]{1,0:T(8,128)(2,1)S(1)}, u32[]{:S(2)}, u32[]{:S(2)}) collective-permute-start(bf16[592,128]{1,0:T(8,128)(2,1)} %get-tuple-element.130), channel_id=1, source_target_pairs={{0,24},{1,25},{2,26},{3,27},{4,28},{5,29},{6,30},{7,31},{8,16},{9,... | collective-permute-start | bytes 454664 | tf_op jit(solution)/shard_map/ppermute | solution.py:1136
  (34 other events, 482.2 us)
